TPU v7x, 32 devices: a whole 2x2x4 slice. The times are simulated.
32 devices in a mesh: grp: 2 (over y), frm: 4 (over z), row: 4 (over x, core).
Axes of the slice: x: 2, y: 2, z: 4, core: 2. Of those that a mesh axis runs over, the one named last changes fastest.
Arguments:
- hidden_in: bfloat16 [512, 16, 2240], P('row', ('grp', 'frm')), parts along dimension 1, may hold values from -6 to 6
- norm_gain: float32 [2240], replicated, may hold values from 0.1 to 1.9
- query_key_value_weight: bfloat16 [2240, 3, 2240], P(None, None, 'row'), may hold values from -0.125 to 0.125
- head_gain: float32 [2240], P('row'), may hold values from 0.1 to 1.9
- output_matrix: bfloat16 [2240, 2240], P('row'), may hold values from -0.125 to 0.125
- block_end: int32 [16], P(('grp', 'frm')), parts along dimension 0, may hold values from 0 to 7, as said below
Outputs:
- mixed_out: bfloat16 [512, 16, 2240], P('row', ('grp', 'frm')), parts along dimension 1
There are 2 independent parts, one for each index of `grp`. A program takes and returns all parts, laid end to end along the dimension named above; an argument that names none is the same for every part. Nothing has to cross between parts.
Inputs may be any that keep to these rules, and one draw needn't show every extreme that they name: `block_end`: entries never fall from one frame to the next; each entry is at least its frame's index, and frames with equal entries form a block of consecutive frames; a block never holds frames of two different runs of 2 frames (f // 2 differs), and the last frame of every such run ends a block.
All inputs are finite; a program needn't handle non-finite values.
Results may differ from a plain program's by a relative error of at most 0.015.
Values may be sent and summed in bfloat16 or wider, within the bound.
No kernel may reach another device: no remote copies, remote signals or barrier semaphores. Data moves between devices by JAX's collectives and lax.ppermute only.
A program may use at most 64 MiB of HBM per device.

v0:
```python
import jax
import jax.numpy as jnp
from jax import lax
from jax.experimental import pallas as pl
from jax.experimental.pallas import tpu as pltpu
from jax.sharding import PartitionSpec as P


HD = 112
EPS = 1e-06
F32 = jnp.float32
BF16 = jnp.bfloat16


def cost(flops, nbytes):
    return pl.CostEstimate(flops=int(flops), bytes_accessed=int(nbytes), transcendentals=0)


def params(mib=24):
    return pltpu.CompilerParams(vmem_limit_bytes=mib << 20)


def dot(a, b):
    return jnp.dot(a, b, preferred_element_type=F32)


def dot_nt(a, b):
    return lax.dot_general(a, b, (((1,), (1,)), ((), ())), preferred_element_type=F32)


VMEM = pl.BlockSpec(memory_space=pltpu.VMEM)


def scaled(x_ref, gain_ref):
    x = x_ref[...].astype(F32)
    mean = jnp.mean(x * x, axis=0, keepdims=True)
    return (x * lax.rsqrt(mean + EPS) * gain_ref[...]).astype(BF16)


def project(blocks, where, gain, weights, states=None, frames=1, first=0, with_query=True, last=False):
    n = len(blocks)
    here, per_frame = len(where), len(where[0])
    features, lanes = blocks[0].shape[-2:]
    group = weights.shape[0] // 3
    heads = group // HD
    width = per_frame * lanes
    total = here * width
    begin = 0 if with_query else group

    def kernel(*refs):
        x_refs, rest = refs[:n], refs[n:]
        gain_ref, w_ref, rest = rest[0], rest[1], rest[2:]
        if states is not None:
            old, rest = rest[0], rest[1:]
        state, second, normed, part = rest[0], rest[1], rest[-2], rest[-1]
        for f in range(here):
            for b, (k, i) in enumerate(where[f]):
                block = x_refs[k] if i is None else x_refs[k].at[i]
                at = f * width + b * lanes
                normed[:, at : at + lanes] = scaled(block, gain_ref)
        part[...] = jnp.dot(w_ref[begin:, :], normed[...], preferred_element_type=F32).astype(BF16)
        keys, values = group - begin, 2 * group - begin
        for f in range(here):
            cols = slice(f * width, (f + 1) * width)
            for h in range(heads):
                k = jnp.maximum(part[keys + h * HD : keys + (h + 1) * HD, cols], 0.0)
                v = part[values + h * HD : values + (h + 1) * HD, cols]
                rows = slice(h * HD, (h + 1) * HD)
                add = dot_nt(v, k)
                state[first + f, rows, :] = add if states is None else old[first + f, rows, :] + add
        if states is not None:
            for f in range(frames):
                if not first <= f < first + here:
                    state[f] = old[f]
        if last:
            own = state[0]
            for f in range(1, frames):
                own = own + state[f]
            second[...] = own.astype(BF16)
        if with_query:
            for f in range(here):
                second[f] = jnp.maximum(part[:group, f * width : (f + 1) * width], 0.0)

    out_shape = [jax.ShapeDtypeStruct((frames, group, HD), F32)]
    scratch = [pltpu.VMEM((3 * group - begin, total), BF16)]
    if last:
        out_shape.append(jax.ShapeDtypeStruct((group, HD), BF16))
    if not with_query:
        out_shape.append(jax.ShapeDtypeStruct((features, total), BF16))
    else:
        out_shape.append(jax.ShapeDtypeStruct((here, group, width), BF16))
        scratch = [pltpu.VMEM((features, total), BF16)] + scratch
    given = [*blocks, gain, weights] + ([] if states is None else [states])
    return pl.pallas_call(
        kernel,
        in_specs=[VMEM] * len(given),
        out_specs=[VMEM] * len(out_shape),
        out_shape=out_shape,
        scratch_shapes=scratch,
        compiler_params=params(),
        cost_estimate=cost(2 * (3 * group - begin) * features * total, 2 * features * total),
        name="project",
    )(*given)


def query(normed, weights, frames):
    features, total = normed.shape
    group = weights.shape[0] // 3
    width = total // frames

    def kernel(x_ref, w_ref, q_ref):
        q = jnp.maximum(dot(w_ref[:group, :], x_ref[...]), 0.0).astype(BF16)
        for f in range(frames):
            q_ref[f] = q[:, f * width : (f + 1) * width]

    return pl.pallas_call(
        kernel,
        in_specs=[VMEM] * 2,
        out_specs=VMEM,
        out_shape=jax.ShapeDtypeStruct((frames, group, width), BF16),
        compiler_params=params(),
        cost_estimate=cost(2 * group * features * total, 2 * features * total),
        name="query",
    )(normed, weights)


def attend(end, states, priors, head_gain, queries, lanes):
    frames, group, _ = states.shape
    heads = group // HD
    n_prior, n_q = len(priors), len(queries)
    places, slabs = [], 0
    seen = {}
    for k, (array, where, first) in enumerate(queries):
        for f, i in where.items():
            for b in range(array.shape[-1] // lanes):
                places.append((k, f, i, b, first + b))
                seen[first + b] = True
    slabs = len(seen)

    def kernel(end_ref, state_ref, gain_ref, *rest):
        prior_refs, q_refs = rest[:n_prior], rest[n_prior : n_prior + n_q]
        outs = rest[n_prior + n_q :]
        prior = jnp.zeros((group, HD), F32)
        for p in prior_refs:
            prior = prior + p[...].astype(F32)
        block = []
        for f in range(frames):
            total = prior
            for g in range(frames):
                seen_by = (end_ref[g] <= end_ref[f]).astype(F32)
                total = total + seen_by * state_ref[g]
            block.append(total.astype(BF16))
        for k, f, i, b, slab in places:
            for h in range(heads):
                rows = slice(h * HD, (h + 1) * HD)
                a = dot(block[f][rows], q_refs[k][i, rows, b * lanes : (b + 1) * lanes])
                mean = jnp.mean(a * a, axis=0, keepdims=True)
                outs[slab][f, rows, :] = (a * lax.rsqrt(mean + EPS) * gain_ref[rows]).astype(BF16)

    return pl.pallas_call(
        kernel,
        in_specs=[pl.BlockSpec(memory_space=pltpu.SMEM)]
        + [pl.BlockSpec(memory_space=pltpu.VMEM)] * (2 + n_prior + n_q),
        out_specs=[pl.BlockSpec(memory_space=pltpu.VMEM)] * slabs,
        out_shape=[jax.ShapeDtypeStruct((frames, group, lanes), BF16)] * slabs,
        compiler_params=params(),
        cost_estimate=cost(2 * group * HD * frames * slabs * lanes, 4 * group * frames * slabs * lanes),
        name="attend",
    )(end, states, head_gain, *priors, *[a for a, _, _ in queries])


def cut(source, start, sizes):
    width = source.shape[-1]

    def kernel(start_ref, src, *rest):
        outs, sem = rest[: len(sizes)], rest[-1]
        copies, at = [], 0
        for k, (out, n) in enumerate(zip(outs, sizes)):
            view = src.at[pl.ds(pl.multiple_of(start_ref[0] + at, 8), n), :]
            copies.append(pltpu.make_async_copy(view, out, sem.at[k]))
            copies[-1].start()
            at += n
        for c in copies:
            c.wait()

    return pl.pallas_call(
        kernel,
        in_specs=[pl.BlockSpec(memory_space=pltpu.SMEM), pl.BlockSpec(memory_space=pl.ANY)],
        out_specs=[VMEM] * len(sizes),
        out_shape=[jax.ShapeDtypeStruct((n, width), source.dtype) for n in sizes],
        scratch_shapes=[pltpu.SemaphoreType.DMA((len(sizes),))],
        compiler_params=params(8),
        cost_estimate=cost(0, 4 * sum(sizes) * width),
        name="cut",
    )(start.reshape(1), source)


def tokens_first(ref):
    return jnp.concatenate([ref[f].T for f in range(ref.shape[0])], axis=0)


def mix(rows, heads_out):
    frames, group, lanes = heads_out[0].shape
    width = rows[0].shape[1]
    n = len(rows)

    def kernel(*refs):
        out = refs[2 * n]
        total = None
        for w, x in zip(refs[:n], refs[n : 2 * n]):
            term = dot(tokens_first(x), w[...])
            total = term if total is None else total + term
        out[...] = total

    return pl.pallas_call(
        kernel,
        in_specs=[VMEM] * (2 * n),
        out_specs=VMEM,
        out_shape=jax.ShapeDtypeStruct((frames * lanes, width), F32),
        compiler_params=params(),
        cost_estimate=cost(4 * width * group * frames * lanes, 4 * width * group),
        name="mix",
    )(*rows, *heads_out)


def copy_rows(refs, matrix, sem, at=0):
    copies = []
    for i, ref in enumerate(refs):
        copies.append(pltpu.make_async_copy(ref, matrix.at[pl.ds(at, ref.shape[0]), :], sem.at[i]))
        copies[-1].start()
        at += ref.shape[0]
    return copies


def add_heads(index, total, parts, shares, matrix=None, ahead=(), room=0):
    heads = []
    for h, _, _, _ in parts:
        if not any(h is other for other in heads):
            heads.append(h)
    frames, group, lanes = heads[0].shape
    share = group // shares
    width = total.shape[1]
    which = [next(i for i, other in enumerate(heads) if other is h) for h, _, _, _ in parts]
    given = [p for _, _, _, pieces in parts for p in pieces]
    given = given if matrix is None else [matrix, given[-1]]
    n, m, n_ahead = len(given), len(heads), len(ahead)
    depth = sum(p.shape[0] for _, _, _, pieces in parts for p in pieces)
    step = 640 if width > 640 else width
    spans = [(a, min(a + step, width)) for a in range(0, width, step)]

    def kernel(index_ref, total_ref, *refs):
        head_refs, piece_refs, refs = refs[:m], refs[m : m + n], refs[m + n :]
        next_refs, out, scratch = refs[:n_ahead], refs[n_ahead], refs[n_ahead + 1 :]
        w = scratch[0] if matrix is not None else scratch[-2]
        if matrix is None:
            waits = copy_rows(piece_refs, w, scratch[-1])
        else:
            waits = copy_rows(piece_refs[1:], w, scratch[-1], depth - given[1].shape[0])
        coming = copy_rows(next_refs, scratch[0], scratch[1]) if ahead else []
        left = []
        for f in range(frames):
            rows = []
            for k, (_, g, first, pieces) in zip(which, parts):
                count = sum(p.shape[0] for p in pieces)
                got = head_refs[k][f, first : first + count, :]
                for t in range(1, shares):
                    there = t * share + first
                    got = jnp.where(index_ref[g] == t, head_refs[k][f, there : there + count, :], got)
                rows.append(got)
            left.append(jnp.concatenate(rows, axis=0).T)
        left = jnp.concatenate(left, axis=0)
        for c in waits:
            c.wait()
        for a, b in spans:
            out[:, a:b] = total_ref[:, a:b] + dot(left, w[:, a:b])
        for c in coming:
            c.wait()

    results, places = [jax.ShapeDtypeStruct(total.shape, F32)], [VMEM]
    scratch = []
    if ahead:
        results.append(pltpu.VMEM((room, width), BF16))
        places.append(VMEM)
        scratch.append(pltpu.SemaphoreType.DMA((n_ahead,)))
    if matrix is not None:
        results.append(pltpu.VMEM(matrix.shape, BF16))
        places.append(VMEM)
        scratch.append(pltpu.SemaphoreType.DMA((1,)))
    else:
        scratch += [pltpu.VMEM((depth, width), BF16), pltpu.SemaphoreType.DMA((n,))]
    anywhere = pl.BlockSpec(memory_space=pl.ANY)
    out = pl.pallas_call(
        kernel,
        in_specs=[pl.BlockSpec(memory_space=pltpu.SMEM)]
        + [VMEM] * (1 + m)
        + [VMEM if v is matrix else anywhere for v in given]
        + [anywhere] * n_ahead,
        out_specs=places,
        out_shape=results,
        scratch_shapes=scratch,
        input_output_aliases={} if matrix is None else {2 + m: 1},
        compiler_params=params(),
        cost_estimate=cost(2 * depth * width * frames * lanes, 2 * depth * width),
        name="add_heads",
    )(index, total, *heads, *given, *ahead)
    return out if ahead else out[0]


def add_last(index, total, parts, shares):
    heads = []
    for h, _, _, _ in parts:
        if not any(h is other for other in heads):
            heads.append(h)
    frames, group, lanes = heads[0].shape
    share = group // shares
    width = total.shape[1]
    which = [next(i for i, other in enumerate(heads) if other is h) for h, _, _, _ in parts]
    given = [p for _, _, _, pieces in parts for p in pieces]
    n, m = len(given), len(heads)
    depth = sum(p.shape[0] for p in given)
    step = 640 if width > 640 else width
    spans = [(a, min(a + step, width)) for a in range(0, width, step)]

    def kernel(index_ref, total_ref, *refs):
        head_refs, piece_refs, (out, w, staged, sem) = refs[:m], refs[m : m + n], refs[m + n :]
        at = 0
        for ref in piece_refs:
            w[at : at + ref.shape[0], :] = ref[...]
            at += ref.shape[0]
        copies = []
        for f in range(frames):
            rows = []
            for k, (_, g, first, pieces) in zip(which, parts):
                count = sum(p.shape[0] for p in pieces)
                got = head_refs[k][f, first : first + count, :]
                for t in range(1, shares):
                    there = t * share + first
                    got = jnp.where(index_ref[g] == t, head_refs[k][f, there : there + count, :], got)
                rows.append(got)
            left = jnp.concatenate(rows, axis=0).T
            here = slice(f * lanes, (f + 1) * lanes)
            for a, b in spans:
                term = total_ref[here, a:b] + dot(left, w[:, a:b])
                staged[f, a:b, :] = term.T.astype(BF16)
            copies.append(pltpu.make_async_copy(staged.at[f], out.at[f], sem.at[f]))
            copies[-1].start()
        for c in copies:
            c.wait()

    shape = (frames, width, lanes)
    return pl.pallas_call(
        kernel,
        in_specs=[pl.BlockSpec(memory_space=pltpu.SMEM)] + [VMEM] * (1 + m + n),
        out_specs=pl.BlockSpec(memory_space=pl.ANY),
        out_shape=jax.ShapeDtypeStruct(shape, BF16),
        scratch_shapes=[
            pltpu.VMEM((depth, width), BF16),
            pltpu.VMEM(shape, BF16),
            pltpu.SemaphoreType.DMA((frames,)),
        ],
        compiler_params=params(),
        cost_estimate=cost(2 * depth * width * frames * lanes, 2 * depth * width),
        name="add_last",
    )(index, total, *heads, *given)


CUTS = (0, 11, 24, 32)
PIECES = len(CUTS) - 1


def per_device(n_grp, n_row, n_frm, hidden_in, norm_gain, qkv_weight, head_gain, output_matrix, block_end):
    def swap(v, k, axis="row"):
        size = {"row": n_row, "grp": n_grp}[axis]
        return lax.ppermute(v, axis, [(i, i ^ k) for i in range(size)])

    def shift(v, s):
        return lax.ppermute(v, "frm", [(i, i + s) for i in range(n_frm - s)])

    lanes, frames, features = hidden_in.shape
    tokens = jnp.transpose(hidden_in, (1, 2, 0))
    weights = jnp.transpose(qkv_weight, (1, 2, 0)).reshape(-1, features)
    gain = norm_gain.reshape(features, 1)
    out_gain = head_gain.reshape(-1, 1)

    pairs = n_row // 2
    crossed = {k: swap(tokens, 2 * k) for k in range(1, pairs)}
    sibling = swap(tokens, 1)
    passed = {k: swap(v, 1) for k, v in crossed.items()}

    where = [[(0, f), (1, f)] for f in range(frames)]
    states, near_q = project([tokens, sibling], where, gain, weights, None, frames)


    group, _ = output_matrix.shape
    grp = lax.axis_index("grp")
    share = group // n_grp
    sizes = [8 * (share // 8 * b // 32 - share // 8 * a // 32) for a, b in zip(CUTS[:-1], CUTS[1:])]
    pieces = cut(output_matrix, grp * share, sizes)
    near_rows = swap(output_matrix, 1)
    index = jnp.stack([grp ^ g for g in range(n_grp)])
    far_rows = []
    for k in range(1, pairs):
        held = {}
        for j, piece in enumerate(pieces):
            held[0, 0, j] = swap(piece, 2 * k)
            for g in range(1, n_grp):
                held[0, g, j] = swap(held[0, 0, j], g, "grp")
            for g in range(n_grp):
                held[1, g, j] = swap(held[0, g, j], 1)
        far_rows.append(held)
    queries = [(near_q, {f: f for f in range(frames)}, 0)]
    waiting = []
    for k in range(1, pairs):
        for c, block in enumerate((crossed[k], passed[k])):
            last = c == 1 and k == pairs - 1
            one = [[(0, f)] for f in range(frames)]
            out = project([block], one, gain, weights, states, frames, 0, False, last)
            states = out[0]
            if last:
                own_sum = out[1]
            waiting.append((out[-1], 2 * k + c))
    if n_frm <= 4:
        priors = [shift(own_sum, s) for s in range(1, n_frm)]
    else:
        total, s = shift(own_sum.astype(F32), 1), 1
        while s < n_frm:
            total, s = total + shift(total, s), 2 * s
        priors = [total]
    for normed, slab in waiting:
        late = query(normed, weights, frames)
        queries.append((late, {f: f for f in range(frames)}, slab))
    heads_out = attend(block_end, states, priors, out_gain, queries, lanes)

    across = []
    for k in range(1, pairs):
        across.append((swap(heads_out[2 * k], 2 * k), swap(heads_out[2 * k + 1], 2 * k + 1)))
    own = mix([output_matrix, near_rows], [heads_out[0], swap(heads_out[1], 1)])
    total, late = own, sum(sizes[:-1])
    for k, (heads, held) in enumerate(zip(across, far_rows)):
        parts = []
        for c in range(2):
            parts.append([(heads[c], 0, 0, [held[c, 0, j] for j in range(PIECES)])])
            parts[c] += [(heads[c], g, 0, [held[c, g, j] for j in range(PIECES - 1)]) for g in range(1, n_grp)]
        ahead = [p for _, _, _, pieces in parts[1] for p in pieces]
        room = sum(p.shape[0] for p in ahead)
        total, matrix = add_heads(index, total, parts[0], n_grp, None, ahead[:-1], room)
        total = add_heads(index, total, parts[1], n_grp, matrix)
        parts = [(heads[c], g, late, [held[c, g, PIECES - 1]]) for c in range(2) for g in range(1, n_grp)]
        if k == pairs - 2:
            total = add_last(index, total, parts, n_grp)
        else:
            total = add_heads(index, total, parts, n_grp)
    return jnp.transpose(total, (2, 0, 1))


def solution(mesh):
    placed = (
        P("row", ("grp", "frm"), None),
        P(),
        P(None, None, "row"),
        P("row"),
        P("row", None),
        P(("grp", "frm")),
    )

    def body(*args):
        return per_device(mesh.shape["grp"], mesh.shape["row"], mesh.shape["frm"], *args)

    return jax.shard_map(
        body, mesh=mesh, in_specs=placed, out_specs=P("row", ("grp", "frm"), None), check_vma=False
    )
```

profile of v0, /device:TPU:0, one launch (start us, length us, event | category | flops | bytes accessed | tf_op | source)
XLA Modules:
  0.0 112.9 jit_solution(864554778634210714)
XLA Ops:
  0.0 3.0 %collective-permute-start.1 = (bf16[2,2240,128]{2,1,0:T(8,128)(2,1)}, bf16[2,2240,128]{2,1,0:T(8,128)(2,1)S(1)}, u32[]{:S(2)}, u32[]{:S(2)}) collective-permute-start(bf16[2,2240,128]{2,1,0:T(8,128)(2,1)} %bitcast.13), channel_id=1, source_target_pairs={{0,2},{1,3},{2,0},{3,1},{4,6},{5,7},{6,4},{7,5},{8,10},{9,11},{10,... | collective-permute-start | bytes 3440648 | tf_op jit(solution)/shard_map/ppermute | solution.py:374
  3.0 0.0 collective-permute-start.3
  3.0 0.5 collective-permute-start
  3.5 25.0 %collective-permute-done.1.refs_0_ = bf16[2,2240,128]{2,1,0:T(8,128)(2,1)S(1)} collective-permute-done((bf16[2,2240,128]{2,1,0:T(8,128)(2,1)}, bf16[2,2240,128]{2,1,0:T(8,128)(2,1)S(1)}, u32[]{:S(2)}, u32[]{:S(2)}) %collective-permute-start.1) | collective-permute-done | bytes 1146912 | tf_op jit(solution)/shard_map/ppermute | solution.py:374
  28.4 0.0 collective-permute-start.2
  28.4 1.7 %copy-done.2 = bf16[560,2240]{1,0:T(8,128)(2,1)S(1)} copy-done((bf16[560,2240]{1,0:T(8,128)(2,1)S(1)}, bf16[560,2240]{1,0:T(8,128)(2,1)}, u32[]{:S(2)}) %copy-start.2) | copy-done | bytes 2508824
  30.2 0.7 cut.1
  30.9 1.8 %collective-permute-start.11 = (bf16[72,2240]{1,0:T(8,128)(2,1)S(1)}, bf16[72,2240]{1,0:T(8,128)(2,1)S(1)}, u32[]{:S(2)}, u32[]{:S(2)}) collective-permute-start(bf16[72,2240]{1,0:T(8,128)(2,1)S(1)} %get-tuple-element.34), channel_id=1, source_target_pairs={{0,2},{1,3},{2,0},{3,1},{4,6},{5,7},{6,4},{7,5},{8,10},{9,11},{10,... | collective-permute-start | bytes 967688 | tf_op jit(solution)/shard_map/ppermute | solution.py:374
  32.7 0.3 collective-permute-start.9
  33.0 0.3 reshape.16.refs_2_.refs_1_
  33.4 8.3 %collective-permute-done.11.refs_3_ = bf16[72,2240]{1,0:T(8,128)(2,1)S(1)} collective-permute-done((bf16[72,2240]{1,0:T(8,128)(2,1)S(1)}, bf16[72,2240]{1,0:T(8,128)(2,1)S(1)}, u32[]{:S(2)}, u32[]{:S(2)}) %collective-permute-start.11) | collective-permute-done | bytes 322592 | tf_op jit(solution)/shard_map/ppermute | solution.py:374
  41.7 1.7 %collective-permute-start.10 = (bf16[112,2240]{1,0:T(8,128)(2,1)S(1)}, bf16[112,2240]{1,0:T(8,128)(2,1)S(1)}, u32[]{:S(2)}, u32[]{:S(2)}) collective-permute-start(bf16[112,2240]{1,0:T(8,128)(2,1)S(1)} %get-tuple-element.33), channel_id=1, source_target_pairs={{0,2},{1,3},{2,0},{3,1},{4,6},{5,7},{6,4},{7,5},{8,10},{9,11},{10,... | collective-permute-start | bytes 1505288 | tf_op jit(solution)/shard_map/ppermute | solution.py:374
  43.4 0.0 collective-permute-done.3.refs_1_
  43.4 0.0 collective-permute-start.16
  43.4 0.0 copy-start
  43.4 3.2 %copy-done = bf16[2240,3,560]{0,2,1:T(8,128)(2,1)S(1)} copy-done((bf16[2240,3,560]{0,2,1:T(8,128)(2,1)S(1)}, bf16[2240,3,560]{0,2,1:T(8,128)(2,1)}, u32[]{:S(2)}) %copy-start) | copy-done | bytes 7526424
  46.6 6.5 %project.3 = (f32[2,560,112]{2,1,0:T(8,128)S(1)}, bf16[2,560,256]{2,1,0:T(8,128)(2,1)S(1)}) custom-call(bf16[2,2240,128]{2,1,0:T(8,128)(2,1)S(1)} %bitcast.15, bf16[2,2240,128]{2,1,0:T(8,128)(2,1)} %collective-permute-done.3.refs_1_, f32[2240,1]{1,0:T(8,128)S(1)} %reshape.16.refs_2_.refs_1_, bf16[1680,2240]{1,0:T(8,128)(2,1)S(1)} %bitcast.8), custom_call_target="tpu_custom_call" | custom-call | flops 3853516800 | bytes 2293760 | tf_op jit(solution)/shard_map/project/pallas_call | solution.py:94
  53.1 0.0 collective-permute-done.2.refs_0_
  53.1 1.6 %collective-permute-start.20 = (bf16[72,2240]{1,0:T(8,128)(2,1)S(1)}, bf16[72,2240]{1,0:T(8,128)(2,1)S(1)}, u32[]{:S(2)}, u32[]{:S(2)}) collective-permute-start(bf16[72,2240]{1,0:T(8,128)(2,1)S(1)} %collective-permute-done.11.refs_3_), channel_id=1, source_target_pairs={{0,16},{16,0},{1,17},{17,1},{2,18},{18,2},{3,19},{19,3},{4,20},{20... | collective-permute-start | bytes 967688 | tf_op jit(solution)/shard_map/ppermute | solution.py:374
  54.7 2.5 %project.4 = (f32[2,560,112]{2,1,0:T(8,128)S(1)}, bf16[2240,256]{1,0:T(8,128)(2,1)S(1)}) custom-call(bf16[2,2240,128]{2,1,0:T(8,128)(2,1)S(1)} %collective-permute-done.1.refs_0_, f32[2240,1]{1,0:T(8,128)S(1)} %reshape.16.refs_2_.refs_1_, bf16[1680,2240]{1,0:T(8,128)(2,1)S(1)} %bitcast.9, f32[2,560,112]{2,1,0:T(8,128)S(1)} %get-tuple-element.22.refs_3_), custom_call_target="tpu_custom_call" | custom-call | flops 1284505600 | bytes 1146880 | tf_op jit(solution)/shard_map/project/pallas_call | solution.py:94
  57.2 0.0 copy-start.21
  57.2 2.5 %project.5 = (f32[2,560,112]{2,1,0:T(8,128)S(1)}, bf16[560,112]{1,0:T(8,128)(2,1)S(1)}, bf16[2240,256]{1,0:T(8,128)(2,1)S(1)}) custom-call(bf16[2,2240,128]{2,1,0:T(8,128)(2,1)S(1)} %collective-permute-done.2.refs_0_, f32[2240,1]{1,0:T(8,128)S(1)} %reshape.16.refs_2_.refs_1_, bf16[1680,2240]{1,0:T(8,128)(2,1)S(1)} %bitcast.10, ...), custom_call_target="tpu_custom_call" | custom-call | flops 1284505600 | bytes 1146880 | tf_op jit(solution)/shard_map/project/pallas_call | solution.py:94
  59.8 0.0 collective-permute-done.9.refs_1_
  59.8 3.5 %collective-permute-start.4 = (bf16[560,112]{1,0:T(8,128)(2,1)S(1)}, bf16[560,112]{1,0:T(8,128)(2,1)S(1)}, u32[]{:S(2)}, u32[]{:S(2)}) collective-permute-start(bf16[560,112]{1,0:T(8,128)(2,1)S(1)} %get-tuple-element.25), channel_id=1, source_target_pairs={{0,4},{4,8},{8,12},{1,5},{5,9},{9,13},{2,6},{6,10},{10,14},{3,7},{... | collective-permute-start | bytes 376328 | tf_op jit(solution)/shard_map/ppermute | solution.py:377
  63.3 0.0 collective-permute-done.10.refs_2_
  63.3 0.0 copy-start.4
  63.3 4.5 %collective-permute-start.5 = (bf16[560,112]{1,0:T(8,128)(2,1)S(1)}, bf16[560,112]{1,0:T(8,128)(2,1)S(1)}, u32[]{:S(2)}, u32[]{:S(2)}) collective-permute-start(bf16[560,112]{1,0:T(8,128)(2,1)S(1)} %get-tuple-element.25), channel_id=1, source_target_pairs={{0,8},{4,12},{1,9},{5,13},{2,10},{6,14},{3,11},{7,15},{16,24},{20,... | collective-permute-start | bytes 376328 | tf_op jit(solution)/shard_map/ppermute | solution.py:377
  67.8 0.0 collective-permute-done.16.refs_8_
  67.8 0.6 collective-permute-start.13
  68.4 0.0 collective-permute-done.20.refs_2_
  68.4 1.5 %collective-permute-start.12 = (bf16[96,2240]{1,0:T(8,128)(2,1)S(1)}, bf16[96,2240]{1,0:T(8,128)(2,1)}, u32[]{:S(2)}, u32[]{:S(2)}) collective-permute-start(bf16[96,2240]{1,0:T(8,128)(2,1)S(1)} %collective-permute-done.9.refs_1_), channel_id=1, source_target_pairs={{0,16},{16,0},{1,17},{17,1},{2,18},{18,2},{3,19},{19,3},{4,20},{20... | collective-permute-start | bytes 1290248 | tf_op jit(solution)/shard_map/ppermute | solution.py:374
  69.9 0.0 collective-permute-done.4.rest_0_
  69.9 4.5 %collective-permute-start.6 = (bf16[560,112]{1,0:T(8,128)(2,1)S(1)}, bf16[560,112]{1,0:T(8,128)(2,1)S(1)}, u32[]{:S(2)}, u32[]{:S(2)}) collective-permute-start(bf16[560,112]{1,0:T(8,128)(2,1)S(1)} %get-tuple-element.25), channel_id=1, source_target_pairs={{0,12},{1,13},{2,14},{3,15},{16,28},{17,29},{18,30},{19,31}} | collective-permute-start | bytes 376328 | tf_op jit(solution)/shard_map/ppermute | solution.py:377
  74.4 0.0 collective-permute-done.5.rest_1_
  74.4 0.1 collective-permute-start.14
  74.5 2.3 %collective-permute-done.6.rest_2_ = bf16[560,112]{1,0:T(8,128)(2,1)S(1)} collective-permute-done((bf16[560,112]{1,0:T(8,128)(2,1)S(1)}, bf16[560,112]{1,0:T(8,128)(2,1)S(1)}, u32[]{:S(2)}, u32[]{:S(2)}) %collective-permute-start.6) | collective-permute-done | bytes 125472 | tf_op jit(solution)/shard_map/ppermute | solution.py:377
  76.9 0.1 reshape.17.gain_ref
  77.0 0.9 query.2.rest_4_
  77.9 0.0 copy-start.18
  77.9 0.0 copy-start.3
  77.9 0.8 query.3.rest_5_
  78.8 2.1 %attend.1 = (bf16[2,560,128]{2,1,0:T(8,128)(2,1)S(1)}, bf16[2,560,128]{2,1,0:T(8,128)(2,1)}, bf16[2,560,128]{2,1,0:T(8,128)(2,1)}, bf16[2,560,128]{2,1,0:T(8,128)(2,1)}) custom-call(s32[2]{0:T(128)S(1)} %copy-done.18, f32[2,560,112]{2,1,0:T(8,128)S(1)} %get-tuple-element.24.state_ref, f32[560,1]{1,0:T(8,128)S(1)} %reshape.17.gain_ref, ...), custom_call_target="tpu_custom_call" | custom-call | flops 128450560 | bytes 2293760 | tf_op jit(solution)/shard_map/attend/pallas_call | solution.py:160
  80.9 0.7 copy-done.16
  81.6 9.2 %collective-permute-done.12.refs_4_ = bf16[96,2240]{1,0:T(8,128)(2,1)} collective-permute-done((bf16[96,2240]{1,0:T(8,128)(2,1)S(1)}, bf16[96,2240]{1,0:T(8,128)(2,1)}, u32[]{:S(2)}, u32[]{:S(2)}) %collective-permute-start.12) | collective-permute-done | bytes 430112 | tf_op jit(solution)/shard_map/ppermute | solution.py:374
  90.8 0.0 collective-permute-start.7
  90.8 0.0 collective-permute-done.13.refs_5_
  90.8 0.5 collective-permute-start.19
  91.3 0.0 collective-permute-done.14.refs_6_
  91.3 0.8 copy-done.10
  92.1 0.0 collective-permute-start.17
  92.1 0.0 collective-permute-done.15.refs_7_
  92.1 0.8 copy-done.6
  92.9 0.5 collective-permute-start.8
  93.4 1.3 %collective-permute-start.18 = (bf16[2,560,128]{2,1,0:T(8,128)(2,1)}, bf16[2,560,128]{2,1,0:T(8,128)(2,1)S(1)}, u32[]{:S(2)}, u32[]{:S(2)}) collective-permute-start(bf16[2,560,128]{2,1,0:T(8,128)(2,1)} %get-tuple-element.36), channel_id=1, source_target_pairs={{0,3},{1,2},{2,1},{3,0},{4,7},{5,6},{6,5},{7,4},{8,11},{9,10},{10,... | collective-permute-start | bytes 860168 | tf_op jit(solution)/shard_map/ppermute | solution.py:374
  94.8 0.3 collective-permute-start.21
  95.0 0.1 pad_add_fusion.index_ref
  95.1 1.0 copy-done.17
  96.1 3.9 %mix.1.total_ref = f32[256,2240]{1,0:T(8,128)S(1)} custom-call(bf16[560,2240]{1,0:T(8,128)(2,1)S(1)} %copy-done.3, bf16[560,2240]{1,0:T(8,128)(2,1)} %collective-permute-done.refs_1_, bf16[2,560,128]{2,1,0:T(8,128)(2,1)S(1)} %copy-done.17, bf16[2,560,128]{2,1,0:T(8,128)(2,1)} %collective-permute-done.7.refs_3_), custom_call_target="tpu_custom_call" | custom-call | flops 1284505600 | bytes 5017600 | tf_op jit(solution)/shard_map/mix/pallas_call | solution.py:215
  100.0 2.8 %collective-permute-done.8.refs_0_ = bf16[2,560,128]{2,1,0:T(8,128)(2,1)S(1)} collective-permute-done((bf16[2,560,128]{2,1,0:T(8,128)(2,1)}, bf16[2,560,128]{2,1,0:T(8,128)(2,1)S(1)}, u32[]{:S(2)}, u32[]{:S(2)}) %collective-permute-start.8) | collective-permute-done | bytes 286752 | tf_op jit(solution)/shard_map/ppermute | solution.py:374
  102.8 3.4 %add_heads.2 = (f32[256,2240]{1,0:T(8,128)S(1)}, bf16[488,2240]{1,0:T(8,128)(2,1)S(1)}) custom-call(s32[2]{0:T(128)S(1)} %pad_add_fusion.index_ref, f32[256,2240]{1,0:T(8,128)S(1)} %mix.1.total_ref, bf16[2,560,128]{2,1,0:T(8,128)(2,1)S(1)} %collective-permute-done.8.refs_0_, bf16[96,2240]{1,0:T(8,128)(2,1)S(1)} %copy-done.9, ...), custom_call_target="tpu_custom_call" | custom-call | flops 559677440 | bytes 2186240 | tf_op jit(solution)/shard_map/add_heads/pallas_call | solution.py:292
  106.3 1.7 %collective-permute-done.18.refs_0_.refs_1_ = bf16[2,560,128]{2,1,0:T(8,128)(2,1)S(1)} collective-permute-done((bf16[2,560,128]{2,1,0:T(8,128)(2,1)}, bf16[2,560,128]{2,1,0:T(8,128)(2,1)S(1)}, u32[]{:S(2)}, u32[]{:S(2)}) %collective-permute-start.18) | collective-permute-done | bytes 286752 | tf_op jit(solution)/shard_map/ppermute | solution.py:374
  108.0 2.5 %add_heads.3 = (f32[256,2240]{1,0:T(8,128)S(1)}, bf16[488,2240]{1,0:T(8,128)(2,1)S(1)}) custom-call(s32[2]{0:T(128)S(1)} %pad_add_fusion.index_ref, f32[256,2240]{1,0:T(8,128)S(1)} %get-tuple-element.35.total_ref, bf16[2,560,128]{2,1,0:T(8,128)(2,1)S(1)} %collective-permute-done.18.refs_0_.refs_1_, ...), custom_call_target="tpu_custom_call", output_to_operand_aliasing={{1}: (3, {})} | custom-call | flops 559677440 | bytes 2186240 | tf_op jit(solution)/shard_map/add_heads/pallas_call | solution.py:292
  110.6 0.0 collective-permute-done.21.refs_3_
  110.6 2.2 %add_last.1 = bf16[2,2240,128]{2,1,0:T(8,128)(2,1)} custom-call(s32[2]{0:T(128)S(1)} %pad_add_fusion.index_ref, f32[256,2240]{1,0:T(8,128)S(1)} %get-tuple-element.38.total_ref, bf16[2,560,128]{2,1,0:T(8,128)(2,1)S(1)} %collective-permute-done.8.refs_0_, bf16[2,560,128]{2,1,0:T(8,128)(2,1)S(1)} %collective-permute-done.18.refs_0_.refs_1_, ...), custom_call_target="tpu_custom_call" | custom-call | flops 165150720 | bytes 645120 | tf_op jit(solution)/shard_map/add_last/pallas_call | solution.py:351
  (38 shorter events, 0.1 us)
Async XLA Ops:
  0.0 33.0 %copy-start.20 = (f32[2240]{0:T(1024)S(1)}, f32[2240]{0:T(1024)}, u32[]{:S(2)}) copy-start(f32[2240]{0:T(1024)} %param.7) | copy-start | bytes 26884
  0.0 28.4 %collective-permute-start.1 = (bf16[2,2240,128]{2,1,0:T(8,128)(2,1)}, bf16[2,2240,128]{2,1,0:T(8,128)(2,1)S(1)}, u32[]{:S(2)}, u32[]{:S(2)}) collective-permute-start(bf16[2,2240,128]{2,1,0:T(8,128)(2,1)} %bitcast.13), channel_id=1, source_target_pairs={{0,2},{1,3},{2,0},{3,1},{4,6},{5,7},{6,4},{7,5},{8,10},{9,11},{10,... | collective-permute-start | bytes 3440648 | tf_op jit(solution)/shard_map/ppermute | solution.py:374
  3.0 40.4 %collective-permute-start.3 = (bf16[2,2240,128]{2,1,0:T(8,128)(2,1)}, bf16[2,2240,128]{2,1,0:T(8,128)(2,1)}, u32[]{:S(2)}, u32[]{:S(2)}) collective-permute-start(bf16[2,2240,128]{2,1,0:T(8,128)(2,1)} %bitcast.14), channel_id=1, source_target_pairs={{0,1},{1,0},{2,3},{3,2},{4,5},{5,4},{6,7},{7,6},{8,9},{9,8},{10,11... | collective-permute-start | bytes 3440648 | tf_op jit(solution)/shard_map/ppermute | solution.py:374
  3.0 90.5 %collective-permute-start = (bf16[560,2240]{1,0:T(8,128)(2,1)}, bf16[560,2240]{1,0:T(8,128)(2,1)}, u32[]{:S(2)}, u32[]{:S(2)}) collective-permute-start(bf16[560,2240]{1,0:T(8,128)(2,1)} %src.1), channel_id=1, source_target_pairs={{0,1},{1,0},{2,3},{3,2},{4,5},{5,4},{6,7},{7,6},{8,9},{9,8},{10,11... | collective-permute-start | bytes 7526408 | tf_op jit(solution)/shard_map/ppermute | solution.py:374
  28.4 24.7 %collective-permute-start.2 = (bf16[2,2240,128]{2,1,0:T(8,128)(2,1)S(1)}, bf16[2,2240,128]{2,1,0:T(8,128)(2,1)S(1)}, u32[]{:S(2)}, u32[]{:S(2)}) collective-permute-start(bf16[2,2240,128]{2,1,0:T(8,128)(2,1)S(1)} %collective-permute-done.1.refs_0_), channel_id=1, source_target_pairs={{0,1},{1,0},{2,3},{3,2},{4,5},{5,4},{6,7},{7,6},{8,9},{9,8},{10,11... | collective-permute-start | bytes 3440648 | tf_op jit(solution)/shard_map/ppermute | solution.py:374
  28.4 1.7 %copy-start.2 = (bf16[560,2240]{1,0:T(8,128)(2,1)S(1)}, bf16[560,2240]{1,0:T(8,128)(2,1)}, u32[]{:S(2)}) copy-start(bf16[560,2240]{1,0:T(8,128)(2,1)} %src.1) | copy-start | bytes 7526404
  30.2 13.2 %copy-start.19 = (bf16[128,2,2240]{0,2,1:T(8,128)(2,1)S(1)}, bf16[128,2,2240]{0,2,1:T(8,128)(2,1)}, u32[]{:S(2)}) copy-start(bf16[128,2,2240]{0,2,1:T(8,128)(2,1)} %param.6) | copy-start | bytes 3440644
  30.9 10.7 %collective-permute-start.11 = (bf16[72,2240]{1,0:T(8,128)(2,1)S(1)}, bf16[72,2240]{1,0:T(8,128)(2,1)S(1)}, u32[]{:S(2)}, u32[]{:S(2)}) collective-permute-start(bf16[72,2240]{1,0:T(8,128)(2,1)S(1)} %get-tuple-element.34), channel_id=1, source_target_pairs={{0,2},{1,3},{2,0},{3,1},{4,6},{5,7},{6,4},{7,5},{8,10},{9,11},{10,... | collective-permute-start | bytes 967688 | tf_op jit(solution)/shard_map/ppermute | solution.py:374
  32.7 27.0 %collective-permute-start.9 = (bf16[96,2240]{1,0:T(8,128)(2,1)S(1)}, bf16[96,2240]{1,0:T(8,128)(2,1)S(1)}, u32[]{:S(2)}, u32[]{:S(2)}) collective-permute-start(bf16[96,2240]{1,0:T(8,128)(2,1)S(1)} %get-tuple-element.32), channel_id=1, source_target_pairs={{0,2},{1,3},{2,0},{3,1},{4,6},{5,7},{6,4},{7,5},{8,10},{9,11},{10,... | collective-permute-start | bytes 1290248 | tf_op jit(solution)/shard_map/ppermute | solution.py:374
  41.7 11.5 %copy-start.12 = (bf16[72,2240]{1,0:T(8,128)(2,1)}, bf16[72,2240]{1,0:T(8,128)(2,1)S(1)}, u32[]{:S(2)}) copy-start(bf16[72,2240]{1,0:T(8,128)(2,1)S(1)} %collective-permute-done.11.refs_3_) | copy-start | bytes 967684
  41.7 21.6 %collective-permute-start.10 = (bf16[112,2240]{1,0:T(8,128)(2,1)S(1)}, bf16[112,2240]{1,0:T(8,128)(2,1)S(1)}, u32[]{:S(2)}, u32[]{:S(2)}) collective-permute-start(bf16[112,2240]{1,0:T(8,128)(2,1)S(1)} %get-tuple-element.33), channel_id=1, source_target_pairs={{0,2},{1,3},{2,0},{3,1},{4,6},{5,7},{6,4},{7,5},{8,10},{9,11},{10,... | collective-permute-start | bytes 1505288 | tf_op jit(solution)/shard_map/ppermute | solution.py:374
  43.4 24.4 %collective-permute-start.16 = (bf16[72,2240]{1,0:T(8,128)(2,1)S(1)}, bf16[72,2240]{1,0:T(8,128)(2,1)S(1)}, u32[]{:S(2)}, u32[]{:S(2)}) collective-permute-start(bf16[72,2240]{1,0:T(8,128)(2,1)S(1)} %collective-permute-done.11.refs_3_), channel_id=1, source_target_pairs={{0,1},{1,0},{2,3},{3,2},{4,5},{5,4},{6,7},{7,6},{8,9},{9,8},{10,11... | collective-permute-start | bytes 967688 | tf_op jit(solution)/shard_map/ppermute | solution.py:374
  43.4 3.2 %copy-start = (bf16[2240,3,560]{0,2,1:T(8,128)(2,1)S(1)}, bf16[2240,3,560]{0,2,1:T(8,128)(2,1)}, u32[]{:S(2)}) copy-start(bf16[2240,3,560]{0,2,1:T(8,128)(2,1)} %param.8) | copy-start | bytes 22579204
  46.6 8.1 %copy-start.1 = (bf16[2240,3,560]{0,2,1:T(8,128)(2,1)S(1)}, bf16[2240,3,560]{0,2,1:T(8,128)(2,1)}, u32[]{:S(2)}) copy-start(bf16[2240,3,560]{0,2,1:T(8,128)(2,1)} %param.8) | copy-start | bytes 22579204
  53.1 15.3 %collective-permute-start.20 = (bf16[72,2240]{1,0:T(8,128)(2,1)S(1)}, bf16[72,2240]{1,0:T(8,128)(2,1)S(1)}, u32[]{:S(2)}, u32[]{:S(2)}) collective-permute-start(bf16[72,2240]{1,0:T(8,128)(2,1)S(1)} %collective-permute-done.11.refs_3_), channel_id=1, source_target_pairs={{0,16},{16,0},{1,17},{17,1},{2,18},{18,2},{3,19},{19,3},{4,20},{20... | collective-permute-start | bytes 967688 | tf_op jit(solution)/shard_map/ppermute | solution.py:374
  57.2 19.6 %copy-start.21 = (f32[560]{0:T(1024)S(1)}, f32[560]{0:T(1024)}, u32[]{:S(2)}) copy-start(f32[560]{0:T(1024)} %param.9) | copy-start | bytes 6724
  59.8 18.1 %copy-start.8 = (bf16[96,2240]{1,0:T(8,128)(2,1)}, bf16[96,2240]{1,0:T(8,128)(2,1)S(1)}, u32[]{:S(2)}) copy-start(bf16[96,2240]{1,0:T(8,128)(2,1)S(1)} %collective-permute-done.9.refs_1_) | copy-start | bytes 1290244
  59.8 10.1 %collective-permute-start.4 = (bf16[560,112]{1,0:T(8,128)(2,1)S(1)}, bf16[560,112]{1,0:T(8,128)(2,1)S(1)}, u32[]{:S(2)}, u32[]{:S(2)}) collective-permute-start(bf16[560,112]{1,0:T(8,128)(2,1)S(1)} %get-tuple-element.25), channel_id=1, source_target_pairs={{0,4},{4,8},{8,12},{1,5},{5,9},{9,13},{2,6},{6,10},{10,14},{3,7},{... | collective-permute-start | bytes 376328 | tf_op jit(solution)/shard_map/ppermute | solution.py:377
  63.3 14.6 %copy-start.4 = (bf16[112,2240]{1,0:T(8,128)(2,1)}, bf16[112,2240]{1,0:T(8,128)(2,1)S(1)}, u32[]{:S(2)}) copy-start(bf16[112,2240]{1,0:T(8,128)(2,1)S(1)} %collective-permute-done.10.refs_2_) | copy-start | bytes 1505284
  63.3 11.1 %collective-permute-start.5 = (bf16[560,112]{1,0:T(8,128)(2,1)S(1)}, bf16[560,112]{1,0:T(8,128)(2,1)S(1)}, u32[]{:S(2)}, u32[]{:S(2)}) collective-permute-start(bf16[560,112]{1,0:T(8,128)(2,1)S(1)} %get-tuple-element.25), channel_id=1, source_target_pairs={{0,8},{4,12},{1,9},{5,13},{2,10},{6,14},{3,11},{7,15},{16,24},{20,... | collective-permute-start | bytes 376328 | tf_op jit(solution)/shard_map/ppermute | solution.py:377
  67.8 10.1 %copy-start.14 = (bf16[72,2240]{1,0:T(8,128)(2,1)}, bf16[72,2240]{1,0:T(8,128)(2,1)S(1)}, u32[]{:S(2)}) copy-start(bf16[72,2240]{1,0:T(8,128)(2,1)S(1)} %collective-permute-done.16.refs_8_) | copy-start | bytes 967684
  67.8 23.0 %collective-permute-start.13 = (bf16[112,2240]{1,0:T(8,128)(2,1)S(1)}, bf16[112,2240]{1,0:T(8,128)(2,1)}, u32[]{:S(2)}, u32[]{:S(2)}) collective-permute-start(bf16[112,2240]{1,0:T(8,128)(2,1)S(1)} %collective-permute-done.10.refs_2_), channel_id=1, source_target_pairs={{0,16},{16,0},{1,17},{17,1},{2,18},{18,2},{3,19},{19,3},{4,20},{20... | collective-permute-start | bytes 1505288 | tf_op jit(solution)/shard_map/ppermute | solution.py:374
  68.4 22.4 %collective-permute-start.12 = (bf16[96,2240]{1,0:T(8,128)(2,1)S(1)}, bf16[96,2240]{1,0:T(8,128)(2,1)}, u32[]{:S(2)}, u32[]{:S(2)}) collective-permute-start(bf16[96,2240]{1,0:T(8,128)(2,1)S(1)} %collective-permute-done.9.refs_1_), channel_id=1, source_target_pairs={{0,16},{16,0},{1,17},{17,1},{2,18},{18,2},{3,19},{19,3},{4,20},{20... | collective-permute-start | bytes 1290248 | tf_op jit(solution)/shard_map/ppermute | solution.py:374
  69.9 6.9 %collective-permute-start.6 = (bf16[560,112]{1,0:T(8,128)(2,1)S(1)}, bf16[560,112]{1,0:T(8,128)(2,1)S(1)}, u32[]{:S(2)}, u32[]{:S(2)}) collective-permute-start(bf16[560,112]{1,0:T(8,128)(2,1)S(1)} %get-tuple-element.25), channel_id=1, source_target_pairs={{0,12},{1,13},{2,14},{3,15},{16,28},{17,29},{18,30},{19,31}} | collective-permute-start | bytes 376328 | tf_op jit(solution)/shard_map/ppermute | solution.py:377
  74.4 16.9 %collective-permute-start.14 = (bf16[96,2240]{1,0:T(8,128)(2,1)S(1)}, bf16[96,2240]{1,0:T(8,128)(2,1)S(1)}, u32[]{:S(2)}, u32[]{:S(2)}) collective-permute-start(bf16[96,2240]{1,0:T(8,128)(2,1)S(1)} %collective-permute-done.9.refs_1_), channel_id=1, source_target_pairs={{0,1},{1,0},{2,3},{3,2},{4,5},{5,4},{6,7},{7,6},{8,9},{9,8},{10,11... | collective-permute-start | bytes 1290248 | tf_op jit(solution)/shard_map/ppermute | solution.py:374
  76.8 15.2 %collective-permute-start.15 = (bf16[112,2240]{1,0:T(8,128)(2,1)S(1)}, bf16[112,2240]{1,0:T(8,128)(2,1)S(1)}, u32[]{:S(2)}, u32[]{:S(2)}) collective-permute-start(bf16[112,2240]{1,0:T(8,128)(2,1)S(1)} %collective-permute-done.10.refs_2_), channel_id=1, source_target_pairs={{0,1},{1,0},{2,3},{3,2},{4,5},{5,4},{6,7},{7,6},{8,9},{9,8},{10,11... | collective-permute-start | bytes 1505288 | tf_op jit(solution)/shard_map/ppermute | solution.py:374
  77.9 0.9 copy-start.18
  77.9 17.2 %copy-start.3 = (bf16[560,2240]{1,0:T(8,128)(2,1)S(1)}, bf16[560,2240]{1,0:T(8,128)(2,1)}, u32[]{:S(2)}) copy-start(bf16[560,2240]{1,0:T(8,128)(2,1)} %src.1) | copy-start | bytes 7526404
  80.9 0.7 copy-start.16
  90.8 4.0 %collective-permute-start.7 = (bf16[2,560,128]{2,1,0:T(8,128)(2,1)}, bf16[2,560,128]{2,1,0:T(8,128)(2,1)}, u32[]{:S(2)}, u32[]{:S(2)}) collective-permute-start(bf16[2,560,128]{2,1,0:T(8,128)(2,1)} %get-tuple-element.30), channel_id=1, source_target_pairs={{0,1},{1,0},{2,3},{3,2},{4,5},{5,4},{6,7},{7,6},{8,9},{9,8},{10,11... | collective-permute-start | bytes 860168 | tf_op jit(solution)/shard_map/ppermute | solution.py:374
  90.8 15.5 %collective-permute-start.19 = (bf16[112,2240]{1,0:T(8,128)(2,1)}, bf16[112,2240]{1,0:T(8,128)(2,1)}, u32[]{:S(2)}, u32[]{:S(2)}) collective-permute-start(bf16[112,2240]{1,0:T(8,128)(2,1)} %collective-permute-done.13.refs_5_), channel_id=1, source_target_pairs={{0,1},{1,0},{2,3},{3,2},{4,5},{5,4},{6,7},{7,6},{8,9},{9,8},{10,11... | collective-permute-start | bytes 1505288 | tf_op jit(solution)/shard_map/ppermute | solution.py:374
  91.3 0.8 copy-start.10
  92.1 7.9 %collective-permute-start.17 = (bf16[96,2240]{1,0:T(8,128)(2,1)}, bf16[96,2240]{1,0:T(8,128)(2,1)}, u32[]{:S(2)}, u32[]{:S(2)}) collective-permute-start(bf16[96,2240]{1,0:T(8,128)(2,1)} %collective-permute-done.12.refs_4_), channel_id=1, source_target_pairs={{0,1},{1,0},{2,3},{3,2},{4,5},{5,4},{6,7},{7,6},{8,9},{9,8},{10,11... | collective-permute-start | bytes 1290248 | tf_op jit(solution)/shard_map/ppermute | solution.py:374
  92.1 0.8 copy-start.6
  92.9 9.9 %collective-permute-start.8 = (bf16[2,560,128]{2,1,0:T(8,128)(2,1)}, bf16[2,560,128]{2,1,0:T(8,128)(2,1)S(1)}, u32[]{:S(2)}, u32[]{:S(2)}) collective-permute-start(bf16[2,560,128]{2,1,0:T(8,128)(2,1)} %get-tuple-element.31), channel_id=1, source_target_pairs={{0,2},{1,3},{2,0},{3,1},{4,6},{5,7},{6,4},{7,5},{8,10},{9,11},{10,... | collective-permute-start | bytes 860168 | tf_op jit(solution)/shard_map/ppermute | solution.py:374
  93.4 14.6 %collective-permute-start.18 = (bf16[2,560,128]{2,1,0:T(8,128)(2,1)}, bf16[2,560,128]{2,1,0:T(8,128)(2,1)S(1)}, u32[]{:S(2)}, u32[]{:S(2)}) collective-permute-start(bf16[2,560,128]{2,1,0:T(8,128)(2,1)} %get-tuple-element.36), channel_id=1, source_target_pairs={{0,3},{1,2},{2,1},{3,0},{4,7},{5,6},{6,5},{7,4},{8,11},{9,10},{10,... | collective-permute-start | bytes 860168 | tf_op jit(solution)/shard_map/ppermute | solution.py:374
  94.8 15.8 %collective-permute-start.21 = (bf16[72,2240]{1,0:T(8,128)(2,1)S(1)}, bf16[72,2240]{1,0:T(8,128)(2,1)S(1)}, u32[]{:S(2)}, u32[]{:S(2)}) collective-permute-start(bf16[72,2240]{1,0:T(8,128)(2,1)S(1)} %collective-permute-done.20.refs_2_), channel_id=1, source_target_pairs={{0,1},{1,0},{2,3},{3,2},{4,5},{5,4},{6,7},{7,6},{8,9},{9,8},{10,11... | collective-permute-start | bytes 967688 | tf_op jit(solution)/shard_map/ppermute | solution.py:374
  95.1 1.0 copy-start.17
  96.1 6.7 %copy-start.5 = (bf16[112,2240]{1,0:T(8,128)(2,1)S(1)}, bf16[112,2240]{1,0:T(8,128)(2,1)}, u32[]{:S(2)}) copy-start(bf16[112,2240]{1,0:T(8,128)(2,1)} %copy-done.4) | copy-start | bytes 1505284
  96.1 6.7 %copy-start.7 = (bf16[112,2240]{1,0:T(8,128)(2,1)S(1)}, bf16[112,2240]{1,0:T(8,128)(2,1)}, u32[]{:S(2)}) copy-start(bf16[112,2240]{1,0:T(8,128)(2,1)} %copy-done.6) | copy-start | bytes 1505284
  96.1 6.7 %copy-start.9 = (bf16[96,2240]{1,0:T(8,128)(2,1)S(1)}, bf16[96,2240]{1,0:T(8,128)(2,1)}, u32[]{:S(2)}) copy-start(bf16[96,2240]{1,0:T(8,128)(2,1)} %copy-done.8) | copy-start | bytes 1290244
  96.1 6.7 %copy-start.11 = (bf16[96,2240]{1,0:T(8,128)(2,1)S(1)}, bf16[96,2240]{1,0:T(8,128)(2,1)}, u32[]{:S(2)}) copy-start(bf16[96,2240]{1,0:T(8,128)(2,1)} %copy-done.10) | copy-start | bytes 1290244
  96.1 6.7 %copy-start.13 = (bf16[72,2240]{1,0:T(8,128)(2,1)S(1)}, bf16[72,2240]{1,0:T(8,128)(2,1)}, u32[]{:S(2)}) copy-start(bf16[72,2240]{1,0:T(8,128)(2,1)} %copy-done.12) | copy-start | bytes 967684
  96.1 6.7 %copy-start.15 = (bf16[72,2240]{1,0:T(8,128)(2,1)S(1)}, bf16[72,2240]{1,0:T(8,128)(2,1)}, u32[]{:S(2)}) copy-start(bf16[72,2240]{1,0:T(8,128)(2,1)} %copy-done.14) | copy-start | bytes 967684
where the time goes:
time: 113 us
  waiting for transfers between devices  49.3 us (44%)
  Pallas kernels  28.1 us (25%)
  starting transfers between devices  26.2 us (23%)
  local copies, waits for them, and re-layouts  8.72 us (8%)
    ppermute x19, waiting for transfers between devices, swap(): return lax.ppermute(v, axis, [(i, i ^ k) for i in range(size)])  47 us
    ppermute x19, starting transfers between devices, swap(): return lax.ppermute(v, axis, [(i, i ^ k) for i in range(size)])  13.7 us
    ppermute x3, starting transfers between devices, shift(): return lax.ppermute(v, 'frm', [(i, i + s) for i in range(n_frm - s)])  12.5 us
    pallas_call x3, Pallas kernels, project(): pl.pallas_call(kernel, in_specs=[VMEM] * len(given), out_specs=[VMEM] * l...  11.5 us
    unnamed x44, local copies, waits for them, and re-layouts  8.24 us
    pallas_call x2, Pallas kernels, add_heads(): pl.pallas_call(kernel, in_specs=[pl.BlockSpec(memory_space=pltpu.SMEM)] +...  5.96 us
    pallas_call x1, Pallas kernels, mix(): pl.pallas_call(kernel, in_specs=[VMEM] * (2 * n), out_specs=VMEM, out_sha...  3.92 us
    ppermute x3, waiting for transfers between devices, shift(): return lax.ppermute(v, 'frm', [(i, i + s) for i in range(n_frm - s)])  2.35 us
  transfers between devices with their start and end apart: 22, of which 6 were waited for; matrix products, arithmetic and copies ran while one was open for 0% of the time, Pallas kernels for 23%

commit v1 on v0

--- a/solution.py
+++ b/solution.py
@@ -223,8 +223,8 @@
     )(*rows, *heads_out)
 
 
-def copy_rows(refs, matrix, sem, at=0):
-    copies = []
+def copy_rows(refs, matrix, sem):
+    copies, at = [], 0
     for i, ref in enumerate(refs):
         copies.append(pltpu.make_async_copy(ref, matrix.at[pl.ds(at, ref.shape[0]), :], sem.at[i]))
         copies[-1].start()
@@ -232,7 +232,7 @@
     return copies
 
 
-def add_heads(index, total, parts, shares, matrix=None, ahead=(), room=0):
+def add_heads(index, total, parts, shares, matrix=None, ahead=()):
     heads = []
     for h, _, _, _ in parts:
         if not any(h is other for other in heads):
@@ -241,21 +241,19 @@
     share = group // shares
     width = total.shape[1]
     which = [next(i for i, other in enumerate(heads) if other is h) for h, _, _, _ in parts]
-    given = [p for _, _, _, pieces in parts for p in pieces]
-    given = given if matrix is None else [matrix, given[-1]]
+    given = [p for _, _, _, pieces in parts for p in pieces] if matrix is None else [matrix]
     n, m, n_ahead = len(given), len(heads), len(ahead)
-    depth = sum(p.shape[0] for _, _, _, pieces in parts for p in pieces)
+    depth = sum(p.shape[0] for p in given)
     step = 640 if width > 640 else width
     spans = [(a, min(a + step, width)) for a in range(0, width, step)]
 
     def kernel(index_ref, total_ref, *refs):
         head_refs, piece_refs, refs = refs[:m], refs[m : m + n], refs[m + n :]
         next_refs, out, scratch = refs[:n_ahead], refs[n_ahead], refs[n_ahead + 1 :]
-        w = scratch[0] if matrix is not None else scratch[-2]
+        w = piece_refs[0] if matrix is not None else scratch[-2]
+        waits = []
         if matrix is None:
             waits = copy_rows(piece_refs, w, scratch[-1])
-        else:
-            waits = copy_rows(piece_refs[1:], w, scratch[-1], depth - given[1].shape[0])
         coming = copy_rows(next_refs, scratch[0], scratch[1]) if ahead else []
         left = []
         for f in range(frames):
@@ -279,26 +277,21 @@
     results, places = [jax.ShapeDtypeStruct(total.shape, F32)], [VMEM]
     scratch = []
     if ahead:
-        results.append(pltpu.VMEM((room, width), BF16))
+        results.append(pltpu.VMEM((sum(p.shape[0] for p in ahead), width), BF16))
         places.append(VMEM)
         scratch.append(pltpu.SemaphoreType.DMA((n_ahead,)))
-    if matrix is not None:
-        results.append(pltpu.VMEM(matrix.shape, BF16))
-        places.append(VMEM)
-        scratch.append(pltpu.SemaphoreType.DMA((1,)))
-    else:
+    if matrix is None:
         scratch += [pltpu.VMEM((depth, width), BF16), pltpu.SemaphoreType.DMA((n,))]
     anywhere = pl.BlockSpec(memory_space=pl.ANY)
     out = pl.pallas_call(
         kernel,
         in_specs=[pl.BlockSpec(memory_space=pltpu.SMEM)]
         + [VMEM] * (1 + m)
-        + [VMEM if v is matrix else anywhere for v in given]
+        + [anywhere if matrix is None else VMEM] * n
         + [anywhere] * n_ahead,
         out_specs=places,
         out_shape=results,
         scratch_shapes=scratch,
-        input_output_aliases={} if matrix is None else {2 + m: 1},
         compiler_params=params(),
         cost_estimate=cost(2 * depth * width * frames * lanes, 2 * depth * width),
         name="add_heads",
@@ -341,7 +334,7 @@
             here = slice(f * lanes, (f + 1) * lanes)
             for a, b in spans:
                 term = total_ref[here, a:b] + dot(left, w[:, a:b])
-                staged[f, a:b, :] = term.T.astype(BF16)
+                staged[f, a:b, :] = term.astype(BF16).T
             copies.append(pltpu.make_async_copy(staged.at[f], out.at[f], sem.at[f]))
             copies[-1].start()
         for c in copies:
@@ -364,7 +357,7 @@
     )(index, total, *heads, *given)
 
 
-CUTS = (0, 11, 24, 32)
+CUTS = (0, 11, 22, 32)
 PIECES = len(CUTS) - 1
 
 
@@ -442,8 +435,7 @@
             parts.append([(heads[c], 0, 0, [held[c, 0, j] for j in range(PIECES)])])
             parts[c] += [(heads[c], g, 0, [held[c, g, j] for j in range(PIECES - 1)]) for g in range(1, n_grp)]
         ahead = [p for _, _, _, pieces in parts[1] for p in pieces]
-        room = sum(p.shape[0] for p in ahead)
-        total, matrix = add_heads(index, total, parts[0], n_grp, None, ahead[:-1], room)
+        total, matrix = add_heads(index, total, parts[0], n_grp, None, ahead)
         total = add_heads(index, total, parts[1], n_grp, matrix)
         parts = [(heads[c], g, late, [held[c, g, PIECES - 1]]) for c in range(2) for g in range(1, n_grp)]
         if k == pairs - 2:

time: 113 us -> 111 us (0.982)
  starting transfers between devices: 26.2 us -> 30.2 us
  waiting for transfers between devices: 49.3 us -> 45.3 us
  Pallas kernels: 28.1 us -> 26.2 us
    ppermute x19, waiting for transfers between devices: 47 us -> 41.9 us  [swap(): return lax.ppermute(v, axis, [(i, i ^ k) for i in range(size)])]
    ppermute x3, starting transfers between devices: 12.5 us -> 16.3 us  [shift(): return lax.ppermute(v, 'frm', [(i, i + s) for i in range(n_frm - s)])]
    pallas_call x3, Pallas kernels: 11.5 us -> 10.1 us  [project(): pl.pallas_call(kernel, in_specs=[VMEM] * len(given), out_specs=[VMEM] * l...]
  transfers between devices with their start and end apart: 22 -> 22, of which waited for: 6 -> 7; matrix products, arithmetic and copies ran while one was open for 0% -> 0% of each run, Pallas kernels for 23% -> 21%
where the time goes in v1:
time: 111 us
  waiting for transfers between devices  45.3 us (41%)
  starting transfers between devices  30.2 us (27%)
  Pallas kernels  26.2 us (24%)
  local copies, waits for them, and re-layouts  8.7 us (8%)
    ppermute x19, waiting for transfers between devices, swap(): return lax.ppermute(v, axis, [(i, i ^ k) for i in range(size)])  41.9 us
    ppermute x3, starting transfers between devices, shift(): return lax.ppermute(v, 'frm', [(i, i + s) for i in range(n_frm - s)])  16.3 us
    ppermute x19, starting transfers between devices, swap(): return lax.ppermute(v, axis, [(i, i ^ k) for i in range(size)])  13.9 us
    pallas_call x3, Pallas kernels, project(): pl.pallas_call(kernel, in_specs=[VMEM] * len(given), out_specs=[VMEM] * l...  10.1 us
    unnamed x44, local copies, waits for them, and re-layouts  8.23 us
    pallas_call x2, Pallas kernels, add_heads(): pl.pallas_call(kernel, in_specs=[pl.BlockSpec(memory_space=pltpu.SMEM)] +...  4.91 us
    pallas_call x1, Pallas kernels, mix(): pl.pallas_call(kernel, in_specs=[VMEM] * (2 * n), out_specs=VMEM, out_sha...  3.92 us
    ppermute x3, waiting for transfers between devices, shift(): return lax.ppermute(v, 'frm', [(i, i + s) for i in range(n_frm - s)])  3.39 us
  transfers between devices with their start and end apart: 22, of which 7 were waited for; matrix products, arithmetic and copies ran while one was open for 0% of the time, Pallas kernels for 21%

profile of v1, /device:TPU:0, one launch (start us, length us, event | category | flops | bytes accessed | tf_op | source)
XLA Modules:
  0.0 110.9 jit_solution(1108661843613449892)
XLA Ops:
  0.0 3.0 %collective-permute-start.1 = (bf16[2,2240,128]{2,1,0:T(8,128)(2,1)}, bf16[2,2240,128]{2,1,0:T(8,128)(2,1)S(1)}, u32[]{:S(2)}, u32[]{:S(2)}) collective-permute-start(bf16[2,2240,128]{2,1,0:T(8,128)(2,1)} %bitcast.13), channel_id=1, source_target_pairs={{0,2},{1,3},{2,0},{3,1},{4,6},{5,7},{6,4},{7,5},{8,10},{9,11},{10,... | collective-permute-start | bytes 3440648 | tf_op jit(solution)/shard_map/ppermute | solution.py:367
  3.0 0.0 collective-permute-start
  3.0 0.5 collective-permute-start.3
  3.5 25.0 %collective-permute-done.1.refs_0_ = bf16[2,2240,128]{2,1,0:T(8,128)(2,1)S(1)} collective-permute-done((bf16[2,2240,128]{2,1,0:T(8,128)(2,1)}, bf16[2,2240,128]{2,1,0:T(8,128)(2,1)S(1)}, u32[]{:S(2)}, u32[]{:S(2)}) %collective-permute-start.1) | collective-permute-done | bytes 1146912 | tf_op jit(solution)/shard_map/ppermute | solution.py:367
  28.4 0.0 collective-permute-start.2
  28.4 1.7 %copy-done.2 = bf16[560,2240]{1,0:T(8,128)(2,1)S(1)} copy-done((bf16[560,2240]{1,0:T(8,128)(2,1)S(1)}, bf16[560,2240]{1,0:T(8,128)(2,1)}, u32[]{:S(2)}) %copy-start.2) | copy-done | bytes 2508824
  30.2 0.7 cut.1
  30.9 0.0 copy-start.19
  30.9 1.8 %collective-permute-start.11 = (bf16[88,2240]{1,0:T(8,128)(2,1)S(1)}, bf16[88,2240]{1,0:T(8,128)(2,1)S(1)}, u32[]{:S(2)}, u32[]{:S(2)}) collective-permute-start(bf16[88,2240]{1,0:T(8,128)(2,1)S(1)} %get-tuple-element.33), channel_id=1, source_target_pairs={{0,2},{1,3},{2,0},{3,1},{4,6},{5,7},{6,4},{7,5},{8,10},{9,11},{10,... | collective-permute-start | bytes 1182728 | tf_op jit(solution)/shard_map/ppermute | solution.py:367
  32.7 0.3 collective-permute-start.9
  33.0 0.3 reshape.16.refs_2_.refs_1_
  33.4 9.9 %collective-permute-done.11.refs_3_ = bf16[88,2240]{1,0:T(8,128)(2,1)S(1)} collective-permute-done((bf16[88,2240]{1,0:T(8,128)(2,1)S(1)}, bf16[88,2240]{1,0:T(8,128)(2,1)S(1)}, u32[]{:S(2)}, u32[]{:S(2)}) %collective-permute-start.11) | collective-permute-done | bytes 394272 | tf_op jit(solution)/shard_map/ppermute | solution.py:367
  43.2 1.7 %collective-permute-start.10 = (bf16[96,2240]{1,0:T(8,128)(2,1)S(1)}, bf16[96,2240]{1,0:T(8,128)(2,1)S(1)}, u32[]{:S(2)}, u32[]{:S(2)}) collective-permute-start(bf16[96,2240]{1,0:T(8,128)(2,1)S(1)} %get-tuple-element.32), channel_id=1, source_target_pairs={{0,2},{1,3},{2,0},{3,1},{4,6},{5,7},{6,4},{7,5},{8,10},{9,11},{10,... | collective-permute-start | bytes 1290248 | tf_op jit(solution)/shard_map/ppermute | solution.py:367
  45.0 0.0 collective-permute-done.3.refs_1_
  45.0 0.0 collective-permute-start.16
  45.0 1.6 %collective-permute-start.20 = (bf16[88,2240]{1,0:T(8,128)(2,1)S(1)}, bf16[88,2240]{1,0:T(8,128)(2,1)}, u32[]{:S(2)}, u32[]{:S(2)}) collective-permute-start(bf16[88,2240]{1,0:T(8,128)(2,1)S(1)} %collective-permute-done.11.refs_3_), channel_id=1, source_target_pairs={{0,16},{16,0},{1,17},{17,1},{2,18},{18,2},{3,19},{19,3},{4,20},{20... | collective-permute-start | bytes 1182728 | tf_op jit(solution)/shard_map/ppermute | solution.py:367
  46.6 3.2 %copy-done = bf16[2240,3,560]{0,2,1:T(8,128)(2,1)S(1)} copy-done((bf16[2240,3,560]{0,2,1:T(8,128)(2,1)S(1)}, bf16[2240,3,560]{0,2,1:T(8,128)(2,1)}, u32[]{:S(2)}) %copy-start) | copy-done | bytes 7526424
  49.8 5.1 %project.3 = (f32[2,560,112]{2,1,0:T(8,128)S(1)}, bf16[2,560,256]{2,1,0:T(8,128)(2,1)S(1)}) custom-call(bf16[2,2240,128]{2,1,0:T(8,128)(2,1)S(1)} %bitcast.15, bf16[2,2240,128]{2,1,0:T(8,128)(2,1)S(1)} %collective-permute-done.3.refs_1_, f32[2240,1]{1,0:T(8,128)S(1)} %reshape.16.refs_2_.refs_1_, bf16[1680,2240]{1,0:T(8,128)(2,1)S(1)} %bitcast.8), custom_call_target="tpu_custom_call" | custom-call | flops 3853516800 | bytes 2293760 | tf_op jit(solution)/shard_map/project/pallas_call | solution.py:94
  54.9 2.5 %project.4 = (f32[2,560,112]{2,1,0:T(8,128)S(1)}, bf16[2240,256]{1,0:T(8,128)(2,1)S(1)}) custom-call(bf16[2,2240,128]{2,1,0:T(8,128)(2,1)S(1)} %collective-permute-done.1.refs_0_, f32[2240,1]{1,0:T(8,128)S(1)} %reshape.16.refs_2_.refs_1_, bf16[1680,2240]{1,0:T(8,128)(2,1)S(1)} %bitcast.9, f32[2,560,112]{2,1,0:T(8,128)S(1)} %get-tuple-element.21.refs_3_), custom_call_target="tpu_custom_call" | custom-call | flops 1284505600 | bytes 1146880 | tf_op jit(solution)/shard_map/project/pallas_call | solution.py:94
  57.4 0.0 copy-start.21
  57.4 2.5 %project.5 = (f32[2,560,112]{2,1,0:T(8,128)S(1)}, bf16[560,112]{1,0:T(8,128)(2,1)S(1)}, bf16[2240,256]{1,0:T(8,128)(2,1)S(1)}) custom-call(bf16[2,2240,128]{2,1,0:T(8,128)(2,1)S(1)} %collective-permute-done.2.refs_0_, f32[2240,1]{1,0:T(8,128)S(1)} %reshape.16.refs_2_.refs_1_, bf16[1680,2240]{1,0:T(8,128)(2,1)S(1)} %bitcast.10, ...), custom_call_target="tpu_custom_call" | custom-call | flops 1284505600 | bytes 1146880 | tf_op jit(solution)/shard_map/project/pallas_call | solution.py:94
  60.0 0.0 copy-start.4
  60.0 3.5 %collective-permute-start.4 = (bf16[560,112]{1,0:T(8,128)(2,1)S(1)}, bf16[560,112]{1,0:T(8,128)(2,1)S(1)}, u32[]{:S(2)}, u32[]{:S(2)}) collective-permute-start(bf16[560,112]{1,0:T(8,128)(2,1)S(1)} %get-tuple-element.24), channel_id=1, source_target_pairs={{0,4},{4,8},{8,12},{1,5},{5,9},{9,13},{2,6},{6,10},{10,14},{3,7},{... | collective-permute-start | bytes 376328 | tf_op jit(solution)/shard_map/ppermute | solution.py:370
  63.5 0.0 collective-permute-done.10.refs_2_
  63.5 4.5 %collective-permute-start.5 = (bf16[560,112]{1,0:T(8,128)(2,1)S(1)}, bf16[560,112]{1,0:T(8,128)(2,1)S(1)}, u32[]{:S(2)}, u32[]{:S(2)}) collective-permute-start(bf16[560,112]{1,0:T(8,128)(2,1)S(1)} %get-tuple-element.24), channel_id=1, source_target_pairs={{0,8},{4,12},{1,9},{5,13},{2,10},{6,14},{3,11},{7,15},{16,24},{20,... | collective-permute-start | bytes 376328 | tf_op jit(solution)/shard_map/ppermute | solution.py:370
  68.0 0.6 collective-permute-start.12
  68.6 0.0 collective-permute-done.20.refs_2_
  68.6 1.5 %collective-permute-start.13 = (bf16[96,2240]{1,0:T(8,128)(2,1)S(1)}, bf16[96,2240]{1,0:T(8,128)(2,1)}, u32[]{:S(2)}, u32[]{:S(2)}) collective-permute-start(bf16[96,2240]{1,0:T(8,128)(2,1)S(1)} %collective-permute-done.10.refs_2_), channel_id=1, source_target_pairs={{0,16},{16,0},{1,17},{17,1},{2,18},{18,2},{3,19},{19,3},{4,20},{20... | collective-permute-start | bytes 1290248 | tf_op jit(solution)/shard_map/ppermute | solution.py:367
  70.1 0.0 collective-permute-done.4.rest_0_
  70.1 0.0 collective-permute-start.14
  70.1 1.0 collective-permute-done.5.rest_1_
  71.1 8.3 %collective-permute-start.6 = (bf16[560,112]{1,0:T(8,128)(2,1)S(1)}, bf16[560,112]{1,0:T(8,128)(2,1)S(1)}, u32[]{:S(2)}, u32[]{:S(2)}) collective-permute-start(bf16[560,112]{1,0:T(8,128)(2,1)S(1)} %get-tuple-element.24), channel_id=1, source_target_pairs={{0,12},{1,13},{2,14},{3,15},{16,28},{17,29},{18,30},{19,31}} | collective-permute-start | bytes 376328 | tf_op jit(solution)/shard_map/ppermute | solution.py:370
  79.4 2.4 %collective-permute-done.6.rest_2_ = bf16[560,112]{1,0:T(8,128)(2,1)S(1)} collective-permute-done((bf16[560,112]{1,0:T(8,128)(2,1)S(1)}, bf16[560,112]{1,0:T(8,128)(2,1)S(1)}, u32[]{:S(2)}, u32[]{:S(2)}) %collective-permute-start.6) | collective-permute-done | bytes 125472 | tf_op jit(solution)/shard_map/ppermute | solution.py:370
  81.8 0.0 collective-permute-start.15
  81.8 0.1 reshape.17.gain_ref
  82.0 0.8 query.2.rest_4_
  82.9 0.0 copy-start.18
  82.9 0.0 copy-start.3
  82.9 0.8 query.3.rest_5_
  83.7 2.1 %attend.1 = (bf16[2,560,128]{2,1,0:T(8,128)(2,1)S(1)}, bf16[2,560,128]{2,1,0:T(8,128)(2,1)S(1)}, bf16[2,560,128]{2,1,0:T(8,128)(2,1)}, bf16[2,560,128]{2,1,0:T(8,128)(2,1)}) custom-call(s32[2]{0:T(128)S(1)} %copy-done.18, f32[2,560,112]{2,1,0:T(8,128)S(1)} %get-tuple-element.23.state_ref, f32[560,1]{1,0:T(8,128)S(1)} %reshape.17.gain_ref, ...), custom_call_target="tpu_custom_call" | custom-call | flops 128450560 | bytes 2293760 | tf_op jit(solution)/shard_map/attend/pallas_call | solution.py:160
  85.9 0.0 collective-permute-done.12.refs_4_
  85.9 0.5 collective-permute-start.7
  86.4 2.9 %collective-permute-done.13.refs_5_ = bf16[96,2240]{1,0:T(8,128)(2,1)} collective-permute-done((bf16[96,2240]{1,0:T(8,128)(2,1)S(1)}, bf16[96,2240]{1,0:T(8,128)(2,1)}, u32[]{:S(2)}, u32[]{:S(2)}) %collective-permute-start.13) | collective-permute-done | bytes 430112 | tf_op jit(solution)/shard_map/ppermute | solution.py:367
  89.3 0.0 collective-permute-start.17
  89.3 0.0 collective-permute-done.14.refs_6_
  89.3 0.8 copy-done.8
  90.1 0.5 collective-permute-start.18
  90.6 0.0 collective-permute-done.15.refs_7_
  90.6 0.8 copy-done.10
  91.4 0.0 collective-permute-start.21
  91.4 0.0 collective-permute-done.refs_1_
  91.4 0.5 collective-permute-start.8
  92.0 0.7 copy-done.16
  92.7 1.3 %collective-permute-start.19 = (bf16[2,560,128]{2,1,0:T(8,128)(2,1)}, bf16[2,560,128]{2,1,0:T(8,128)(2,1)S(1)}, u32[]{:S(2)}, u32[]{:S(2)}) collective-permute-start(bf16[2,560,128]{2,1,0:T(8,128)(2,1)} %get-tuple-element.35), channel_id=1, source_target_pairs={{0,3},{1,2},{2,1},{3,0},{4,7},{5,6},{6,5},{7,4},{8,11},{9,10},{10,... | collective-permute-start | bytes 860168 | tf_op jit(solution)/shard_map/ppermute | solution.py:367
  94.0 0.1 pad_add_fusion.index_ref
  94.1 1.0 copy-done.17
  95.1 3.9 %mix.1.total_ref = f32[256,2240]{1,0:T(8,128)S(1)} custom-call(bf16[560,2240]{1,0:T(8,128)(2,1)S(1)} %copy-done.3, bf16[560,2240]{1,0:T(8,128)(2,1)} %collective-permute-done.refs_1_, bf16[2,560,128]{2,1,0:T(8,128)(2,1)S(1)} %get-tuple-element.28.refs_2_, bf16[2,560,128]{2,1,0:T(8,128)(2,1)S(1)} %copy-done.17), custom_call_target="tpu_custom_call" | custom-call | flops 1284505600 | bytes 5017600 | tf_op jit(solution)/shard_map/mix/pallas_call | solution.py:215
  99.0 0.0 collective-permute-done.18.refs_10_
  99.0 2.3 %collective-permute-done.8.refs_0_ = bf16[2,560,128]{2,1,0:T(8,128)(2,1)S(1)} collective-permute-done((bf16[2,560,128]{2,1,0:T(8,128)(2,1)}, bf16[2,560,128]{2,1,0:T(8,128)(2,1)S(1)}, u32[]{:S(2)}, u32[]{:S(2)}) %collective-permute-start.8) | collective-permute-done | bytes 286752 | tf_op jit(solution)/shard_map/ppermute | solution.py:367
  101.4 3.4 %add_heads.2 = (f32[256,2240]{1,0:T(8,128)S(1)}, bf16[472,2240]{1,0:T(8,128)(2,1)S(1)}) custom-call(s32[2]{0:T(128)S(1)} %pad_add_fusion.index_ref, f32[256,2240]{1,0:T(8,128)S(1)} %mix.1.total_ref, bf16[2,560,128]{2,1,0:T(8,128)(2,1)S(1)} %collective-permute-done.8.refs_0_, bf16[96,2240]{1,0:T(8,128)(2,1)S(1)} %copy-done.5, bf16[96,2240]{1,0:T(8,128)(2,1)S(1)} %copy-done.7, ...), custom_call_target="tpu_custom_call" | custom-call | flops 541327360 | bytes 2114560 | tf_op jit(solution)/shard_map/add_heads/pallas_call | solution.py:286
  104.8 1.8 %collective-permute-done.19.refs_0_.refs_1_ = bf16[2,560,128]{2,1,0:T(8,128)(2,1)S(1)} collective-permute-done((bf16[2,560,128]{2,1,0:T(8,128)(2,1)}, bf16[2,560,128]{2,1,0:T(8,128)(2,1)S(1)}, u32[]{:S(2)}, u32[]{:S(2)}) %collective-permute-start.19) | collective-permute-done | bytes 286752 | tf_op jit(solution)/shard_map/ppermute | solution.py:367
  106.5 1.5 %add_heads.3.total_ref = f32[256,2240]{1,0:T(8,128)S(1)} custom-call(s32[2]{0:T(128)S(1)} %pad_add_fusion.index_ref, f32[256,2240]{1,0:T(8,128)S(1)} %get-tuple-element.34.total_ref, bf16[2,560,128]{2,1,0:T(8,128)(2,1)S(1)} %collective-permute-done.19.refs_0_.refs_1_, bf16[472,2240]{1,0:T(8,128)(2,1)S(1)} %get-tuple-element.36.refs_1_), custom_call_target="tpu_custom_call" | custom-call | flops 541327360 | bytes 2114560 | tf_op jit(solution)/shard_map/add_heads/pallas_call | solution.py:286
  108.1 0.0 collective-permute-done.21.refs_3_
  108.1 2.7 %add_last.1 = bf16[2,2240,128]{2,1,0:T(8,128)(2,1)} custom-call(s32[2]{0:T(128)S(1)} %pad_add_fusion.index_ref, f32[256,2240]{1,0:T(8,128)S(1)} %add_heads.3.total_ref, bf16[2,560,128]{2,1,0:T(8,128)(2,1)S(1)} %collective-permute-done.8.refs_0_, bf16[2,560,128]{2,1,0:T(8,128)(2,1)S(1)} %collective-permute-done.19.refs_0_.refs_1_, ...), custom_call_target="tpu_custom_call" | custom-call | flops 201850880 | bytes 788480 | tf_op jit(solution)/shard_map/add_last/pallas_call | solution.py:344
  (38 shorter events, 0.1 us)
Async XLA Ops:
  0.0 28.4 %collective-permute-start.1 = (bf16[2,2240,128]{2,1,0:T(8,128)(2,1)}, bf16[2,2240,128]{2,1,0:T(8,128)(2,1)S(1)}, u32[]{:S(2)}, u32[]{:S(2)}) collective-permute-start(bf16[2,2240,128]{2,1,0:T(8,128)(2,1)} %bitcast.13), channel_id=1, source_target_pairs={{0,2},{1,3},{2,0},{3,1},{4,6},{5,7},{6,4},{7,5},{8,10},{9,11},{10,... | collective-permute-start | bytes 3440648 | tf_op jit(solution)/shard_map/ppermute | solution.py:367
  3.0 88.4 %collective-permute-start = (bf16[560,2240]{1,0:T(8,128)(2,1)}, bf16[560,2240]{1,0:T(8,128)(2,1)}, u32[]{:S(2)}, u32[]{:S(2)}) collective-permute-start(bf16[560,2240]{1,0:T(8,128)(2,1)} %src.1), channel_id=1, source_target_pairs={{0,1},{1,0},{2,3},{3,2},{4,5},{5,4},{6,7},{7,6},{8,9},{9,8},{10,11... | collective-permute-start | bytes 7526408 | tf_op jit(solution)/shard_map/ppermute | solution.py:367
  3.0 42.0 %collective-permute-start.3 = (bf16[2,2240,128]{2,1,0:T(8,128)(2,1)}, bf16[2,2240,128]{2,1,0:T(8,128)(2,1)S(1)}, u32[]{:S(2)}, u32[]{:S(2)}) collective-permute-start(bf16[2,2240,128]{2,1,0:T(8,128)(2,1)} %bitcast.14), channel_id=1, source_target_pairs={{0,1},{1,0},{2,3},{3,2},{4,5},{5,4},{6,7},{7,6},{8,9},{9,8},{10,11... | collective-permute-start | bytes 3440648 | tf_op jit(solution)/shard_map/ppermute | solution.py:367
  28.4 16.6 %collective-permute-start.2 = (bf16[2,2240,128]{2,1,0:T(8,128)(2,1)S(1)}, bf16[2,2240,128]{2,1,0:T(8,128)(2,1)S(1)}, u32[]{:S(2)}, u32[]{:S(2)}) collective-permute-start(bf16[2,2240,128]{2,1,0:T(8,128)(2,1)S(1)} %collective-permute-done.1.refs_0_), channel_id=1, source_target_pairs={{0,1},{1,0},{2,3},{3,2},{4,5},{5,4},{6,7},{7,6},{8,9},{9,8},{10,11... | collective-permute-start | bytes 3440648 | tf_op jit(solution)/shard_map/ppermute | solution.py:367
  28.4 1.7 %copy-start.2 = (bf16[560,2240]{1,0:T(8,128)(2,1)S(1)}, bf16[560,2240]{1,0:T(8,128)(2,1)}, u32[]{:S(2)}) copy-start(bf16[560,2240]{1,0:T(8,128)(2,1)} %src.1) | copy-start | bytes 7526404
  30.2 2.9 %copy-start.20 = (f32[2240]{0:T(1024)S(1)}, f32[2240]{0:T(1024)}, u32[]{:S(2)}) copy-start(f32[2240]{0:T(1024)} %param.7) | copy-start | bytes 26884
  30.9 15.7 %copy-start.19 = (bf16[128,2,2240]{0,2,1:T(8,128)(2,1)S(1)}, bf16[128,2,2240]{0,2,1:T(8,128)(2,1)}, u32[]{:S(2)}) copy-start(bf16[128,2,2240]{0,2,1:T(8,128)(2,1)} %param.6) | copy-start | bytes 3440644
  30.9 12.3 %collective-permute-start.11 = (bf16[88,2240]{1,0:T(8,128)(2,1)S(1)}, bf16[88,2240]{1,0:T(8,128)(2,1)S(1)}, u32[]{:S(2)}, u32[]{:S(2)}) collective-permute-start(bf16[88,2240]{1,0:T(8,128)(2,1)S(1)} %get-tuple-element.33), channel_id=1, source_target_pairs={{0,2},{1,3},{2,0},{3,1},{4,6},{5,7},{6,4},{7,5},{8,10},{9,11},{10,... | collective-permute-start | bytes 1182728 | tf_op jit(solution)/shard_map/ppermute | solution.py:367
  32.7 27.2 %collective-permute-start.9 = (bf16[96,2240]{1,0:T(8,128)(2,1)S(1)}, bf16[96,2240]{1,0:T(8,128)(2,1)S(1)}, u32[]{:S(2)}, u32[]{:S(2)}) collective-permute-start(bf16[96,2240]{1,0:T(8,128)(2,1)S(1)} %get-tuple-element.31), channel_id=1, source_target_pairs={{0,2},{1,3},{2,0},{3,1},{4,6},{5,7},{6,4},{7,5},{8,10},{9,11},{10,... | collective-permute-start | bytes 1290248 | tf_op jit(solution)/shard_map/ppermute | solution.py:367
  43.2 11.6 %copy-start.12 = (bf16[88,2240]{1,0:T(8,128)(2,1)}, bf16[88,2240]{1,0:T(8,128)(2,1)S(1)}, u32[]{:S(2)}) copy-start(bf16[88,2240]{1,0:T(8,128)(2,1)S(1)} %collective-permute-done.11.refs_3_) | copy-start | bytes 1182724
  43.2 20.2 %collective-permute-start.10 = (bf16[96,2240]{1,0:T(8,128)(2,1)S(1)}, bf16[96,2240]{1,0:T(8,128)(2,1)S(1)}, u32[]{:S(2)}, u32[]{:S(2)}) collective-permute-start(bf16[96,2240]{1,0:T(8,128)(2,1)S(1)} %get-tuple-element.32), channel_id=1, source_target_pairs={{0,2},{1,3},{2,0},{3,1},{4,6},{5,7},{6,4},{7,5},{8,10},{9,11},{10,... | collective-permute-start | bytes 1290248 | tf_op jit(solution)/shard_map/ppermute | solution.py:367
  45.0 23.0 %collective-permute-start.16 = (bf16[88,2240]{1,0:T(8,128)(2,1)S(1)}, bf16[88,2240]{1,0:T(8,128)(2,1)S(1)}, u32[]{:S(2)}, u32[]{:S(2)}) collective-permute-start(bf16[88,2240]{1,0:T(8,128)(2,1)S(1)} %collective-permute-done.11.refs_3_), channel_id=1, source_target_pairs={{0,1},{1,0},{2,3},{3,2},{4,5},{5,4},{6,7},{7,6},{8,9},{9,8},{10,11... | collective-permute-start | bytes 1182728 | tf_op jit(solution)/shard_map/ppermute | solution.py:367
  45.0 23.6 %collective-permute-start.20 = (bf16[88,2240]{1,0:T(8,128)(2,1)S(1)}, bf16[88,2240]{1,0:T(8,128)(2,1)}, u32[]{:S(2)}, u32[]{:S(2)}) collective-permute-start(bf16[88,2240]{1,0:T(8,128)(2,1)S(1)} %collective-permute-done.11.refs_3_), channel_id=1, source_target_pairs={{0,16},{16,0},{1,17},{17,1},{2,18},{18,2},{3,19},{19,3},{4,20},{20... | collective-permute-start | bytes 1182728 | tf_op jit(solution)/shard_map/ppermute | solution.py:367
  46.6 3.2 %copy-start = (bf16[2240,3,560]{0,2,1:T(8,128)(2,1)S(1)}, bf16[2240,3,560]{0,2,1:T(8,128)(2,1)}, u32[]{:S(2)}) copy-start(bf16[2240,3,560]{0,2,1:T(8,128)(2,1)} %param.8) | copy-start | bytes 22579204
  49.8 5.1 %copy-start.1 = (bf16[2240,3,560]{0,2,1:T(8,128)(2,1)S(1)}, bf16[2240,3,560]{0,2,1:T(8,128)(2,1)}, u32[]{:S(2)}) copy-start(bf16[2240,3,560]{0,2,1:T(8,128)(2,1)} %param.8) | copy-start | bytes 22579204
  57.4 24.5 %copy-start.21 = (f32[560]{0:T(1024)S(1)}, f32[560]{0:T(1024)}, u32[]{:S(2)}) copy-start(f32[560]{0:T(1024)} %param.9) | copy-start | bytes 6724
  60.0 22.9 %copy-start.4 = (bf16[96,2240]{1,0:T(8,128)(2,1)}, bf16[96,2240]{1,0:T(8,128)(2,1)S(1)}, u32[]{:S(2)}) copy-start(bf16[96,2240]{1,0:T(8,128)(2,1)S(1)} %collective-permute-done.9.refs_1_) | copy-start | bytes 1290244
  60.0 10.1 %collective-permute-start.4 = (bf16[560,112]{1,0:T(8,128)(2,1)S(1)}, bf16[560,112]{1,0:T(8,128)(2,1)S(1)}, u32[]{:S(2)}, u32[]{:S(2)}) collective-permute-start(bf16[560,112]{1,0:T(8,128)(2,1)S(1)} %get-tuple-element.24), channel_id=1, source_target_pairs={{0,4},{4,8},{8,12},{1,5},{5,9},{9,13},{2,6},{6,10},{10,14},{3,7},{... | collective-permute-start | bytes 376328 | tf_op jit(solution)/shard_map/ppermute | solution.py:370
  63.5 19.4 %copy-start.6 = (bf16[96,2240]{1,0:T(8,128)(2,1)}, bf16[96,2240]{1,0:T(8,128)(2,1)S(1)}, u32[]{:S(2)}) copy-start(bf16[96,2240]{1,0:T(8,128)(2,1)S(1)} %collective-permute-done.10.refs_2_) | copy-start | bytes 1290244
  63.5 7.6 %collective-permute-start.5 = (bf16[560,112]{1,0:T(8,128)(2,1)S(1)}, bf16[560,112]{1,0:T(8,128)(2,1)S(1)}, u32[]{:S(2)}, u32[]{:S(2)}) collective-permute-start(bf16[560,112]{1,0:T(8,128)(2,1)S(1)} %get-tuple-element.24), channel_id=1, source_target_pairs={{0,8},{4,12},{1,9},{5,13},{2,10},{6,14},{3,11},{7,15},{16,24},{20,... | collective-permute-start | bytes 376328 | tf_op jit(solution)/shard_map/ppermute | solution.py:370
  68.0 14.9 %copy-start.14 = (bf16[88,2240]{1,0:T(8,128)(2,1)}, bf16[88,2240]{1,0:T(8,128)(2,1)S(1)}, u32[]{:S(2)}) copy-start(bf16[88,2240]{1,0:T(8,128)(2,1)S(1)} %collective-permute-done.16.refs_8_) | copy-start | bytes 1182724
  68.0 17.9 %collective-permute-start.12 = (bf16[96,2240]{1,0:T(8,128)(2,1)S(1)}, bf16[96,2240]{1,0:T(8,128)(2,1)}, u32[]{:S(2)}, u32[]{:S(2)}) collective-permute-start(bf16[96,2240]{1,0:T(8,128)(2,1)S(1)} %collective-permute-done.9.refs_1_), channel_id=1, source_target_pairs={{0,16},{16,0},{1,17},{17,1},{2,18},{18,2},{3,19},{19,3},{4,20},{20... | collective-permute-start | bytes 1290248 | tf_op jit(solution)/shard_map/ppermute | solution.py:367
  68.6 20.8 %collective-permute-start.13 = (bf16[96,2240]{1,0:T(8,128)(2,1)S(1)}, bf16[96,2240]{1,0:T(8,128)(2,1)}, u32[]{:S(2)}, u32[]{:S(2)}) collective-permute-start(bf16[96,2240]{1,0:T(8,128)(2,1)S(1)} %collective-permute-done.10.refs_2_), channel_id=1, source_target_pairs={{0,16},{16,0},{1,17},{17,1},{2,18},{18,2},{3,19},{19,3},{4,20},{20... | collective-permute-start | bytes 1290248 | tf_op jit(solution)/shard_map/ppermute | solution.py:367
  70.1 19.2 %collective-permute-start.14 = (bf16[96,2240]{1,0:T(8,128)(2,1)S(1)}, bf16[96,2240]{1,0:T(8,128)(2,1)S(1)}, u32[]{:S(2)}, u32[]{:S(2)}) collective-permute-start(bf16[96,2240]{1,0:T(8,128)(2,1)S(1)} %collective-permute-done.9.refs_1_), channel_id=1, source_target_pairs={{0,1},{1,0},{2,3},{3,2},{4,5},{5,4},{6,7},{7,6},{8,9},{9,8},{10,11... | collective-permute-start | bytes 1290248 | tf_op jit(solution)/shard_map/ppermute | solution.py:367
  71.1 10.8 %collective-permute-start.6 = (bf16[560,112]{1,0:T(8,128)(2,1)S(1)}, bf16[560,112]{1,0:T(8,128)(2,1)S(1)}, u32[]{:S(2)}, u32[]{:S(2)}) collective-permute-start(bf16[560,112]{1,0:T(8,128)(2,1)S(1)} %get-tuple-element.24), channel_id=1, source_target_pairs={{0,12},{1,13},{2,14},{3,15},{16,28},{17,29},{18,30},{19,31}} | collective-permute-start | bytes 376328 | tf_op jit(solution)/shard_map/ppermute | solution.py:370
  81.8 8.8 %collective-permute-start.15 = (bf16[96,2240]{1,0:T(8,128)(2,1)S(1)}, bf16[96,2240]{1,0:T(8,128)(2,1)S(1)}, u32[]{:S(2)}, u32[]{:S(2)}) collective-permute-start(bf16[96,2240]{1,0:T(8,128)(2,1)S(1)} %collective-permute-done.10.refs_2_), channel_id=1, source_target_pairs={{0,1},{1,0},{2,3},{3,2},{4,5},{5,4},{6,7},{7,6},{8,9},{9,8},{10,11... | collective-permute-start | bytes 1290248 | tf_op jit(solution)/shard_map/ppermute | solution.py:367
  82.9 0.9 copy-start.18
  82.9 11.2 %copy-start.3 = (bf16[560,2240]{1,0:T(8,128)(2,1)S(1)}, bf16[560,2240]{1,0:T(8,128)(2,1)}, u32[]{:S(2)}) copy-start(bf16[560,2240]{1,0:T(8,128)(2,1)} %src.1) | copy-start | bytes 7526404
  85.9 6.1 %collective-permute-start.7 = (bf16[2,560,128]{2,1,0:T(8,128)(2,1)S(1)}, bf16[2,560,128]{2,1,0:T(8,128)(2,1)S(1)}, u32[]{:S(2)}, u32[]{:S(2)}) collective-permute-start(bf16[2,560,128]{2,1,0:T(8,128)(2,1)S(1)} %get-tuple-element.29), channel_id=1, source_target_pairs={{0,1},{1,0},{2,3},{3,2},{4,5},{5,4},{6,7},{7,6},{8,9},{9,8},{10,11... | collective-permute-start | bytes 860168 | tf_op jit(solution)/shard_map/ppermute | solution.py:367
  89.3 9.7 %collective-permute-start.17 = (bf16[96,2240]{1,0:T(8,128)(2,1)}, bf16[96,2240]{1,0:T(8,128)(2,1)}, u32[]{:S(2)}, u32[]{:S(2)}) collective-permute-start(bf16[96,2240]{1,0:T(8,128)(2,1)} %collective-permute-done.12.refs_4_), channel_id=1, source_target_pairs={{0,1},{1,0},{2,3},{3,2},{4,5},{5,4},{6,7},{7,6},{8,9},{9,8},{10,11... | collective-permute-start | bytes 1290248 | tf_op jit(solution)/shard_map/ppermute | solution.py:367
  89.3 0.8 copy-start.8
  90.1 8.9 %collective-permute-start.18 = (bf16[96,2240]{1,0:T(8,128)(2,1)}, bf16[96,2240]{1,0:T(8,128)(2,1)}, u32[]{:S(2)}, u32[]{:S(2)}) collective-permute-start(bf16[96,2240]{1,0:T(8,128)(2,1)} %collective-permute-done.13.refs_5_), channel_id=1, source_target_pairs={{0,1},{1,0},{2,3},{3,2},{4,5},{5,4},{6,7},{7,6},{8,9},{9,8},{10,11... | collective-permute-start | bytes 1290248 | tf_op jit(solution)/shard_map/ppermute | solution.py:367
  90.6 0.8 copy-start.10
  91.4 16.7 %collective-permute-start.21 = (bf16[88,2240]{1,0:T(8,128)(2,1)}, bf16[88,2240]{1,0:T(8,128)(2,1)}, u32[]{:S(2)}, u32[]{:S(2)}) collective-permute-start(bf16[88,2240]{1,0:T(8,128)(2,1)} %collective-permute-done.20.refs_2_), channel_id=1, source_target_pairs={{0,1},{1,0},{2,3},{3,2},{4,5},{5,4},{6,7},{7,6},{8,9},{9,8},{10,11... | collective-permute-start | bytes 1182728 | tf_op jit(solution)/shard_map/ppermute | solution.py:367
  91.4 9.9 %collective-permute-start.8 = (bf16[2,560,128]{2,1,0:T(8,128)(2,1)}, bf16[2,560,128]{2,1,0:T(8,128)(2,1)S(1)}, u32[]{:S(2)}, u32[]{:S(2)}) collective-permute-start(bf16[2,560,128]{2,1,0:T(8,128)(2,1)} %get-tuple-element.30), channel_id=1, source_target_pairs={{0,2},{1,3},{2,0},{3,1},{4,6},{5,7},{6,4},{7,5},{8,10},{9,11},{10,... | collective-permute-start | bytes 860168 | tf_op jit(solution)/shard_map/ppermute | solution.py:367
  92.0 0.7 copy-start.16
  92.7 13.9 %collective-permute-start.19 = (bf16[2,560,128]{2,1,0:T(8,128)(2,1)}, bf16[2,560,128]{2,1,0:T(8,128)(2,1)S(1)}, u32[]{:S(2)}, u32[]{:S(2)}) collective-permute-start(bf16[2,560,128]{2,1,0:T(8,128)(2,1)} %get-tuple-element.35), channel_id=1, source_target_pairs={{0,3},{1,2},{2,1},{3,0},{4,7},{5,6},{6,5},{7,4},{8,11},{9,10},{10,... | collective-permute-start | bytes 860168 | tf_op jit(solution)/shard_map/ppermute | solution.py:367
  94.1 1.0 copy-start.17
  95.0 6.3 %copy-start.5 = (bf16[96,2240]{1,0:T(8,128)(2,1)S(1)}, bf16[96,2240]{1,0:T(8,128)(2,1)}, u32[]{:S(2)}) copy-start(bf16[96,2240]{1,0:T(8,128)(2,1)} %copy-done.4) | copy-start | bytes 1290244
  95.0 6.3 %copy-start.7 = (bf16[96,2240]{1,0:T(8,128)(2,1)S(1)}, bf16[96,2240]{1,0:T(8,128)(2,1)}, u32[]{:S(2)}) copy-start(bf16[96,2240]{1,0:T(8,128)(2,1)} %copy-done.6) | copy-start | bytes 1290244
  95.0 6.3 %copy-start.9 = (bf16[96,2240]{1,0:T(8,128)(2,1)S(1)}, bf16[96,2240]{1,0:T(8,128)(2,1)}, u32[]{:S(2)}) copy-start(bf16[96,2240]{1,0:T(8,128)(2,1)} %copy-done.8) | copy-start | bytes 1290244
  95.0 6.3 %copy-start.11 = (bf16[96,2240]{1,0:T(8,128)(2,1)S(1)}, bf16[96,2240]{1,0:T(8,128)(2,1)}, u32[]{:S(2)}) copy-start(bf16[96,2240]{1,0:T(8,128)(2,1)} %copy-done.10) | copy-start | bytes 1290244
  95.0 6.3 %copy-start.13 = (bf16[88,2240]{1,0:T(8,128)(2,1)S(1)}, bf16[88,2240]{1,0:T(8,128)(2,1)}, u32[]{:S(2)}) copy-start(bf16[88,2240]{1,0:T(8,128)(2,1)} %copy-done.12) | copy-start | bytes 1182724
  95.1 6.3 %copy-start.15 = (bf16[88,2240]{1,0:T(8,128)(2,1)S(1)}, bf16[88,2240]{1,0:T(8,128)(2,1)}, u32[]{:S(2)}) copy-start(bf16[88,2240]{1,0:T(8,128)(2,1)} %copy-done.14) | copy-start | bytes 1182724
